TPU v7x, 32 devices: a whole 2x2x4 slice. The times are simulated.
32 devices in a mesh: dp: 8 (over y, x, core), tensor: 4 (over z).
Axes of the slice: x: 2, y: 2, z: 4, core: 2. Of those that a mesh axis runs over, the one named last changes fastest.
Arguments:
- tokens: bfloat16 [12288, 768], P('dp'), may hold values from -6 to 6
- cotangent: bfloat16 [12288, 768], P('dp'), may hold values from -6 to 6
- dealing: int32 [12288], P('dp'), may hold values from 0 to 12287, as said below
- segments: int32 [8, 1536], P('dp'), may hold values from 0 to 7, never falling along the last dimension, each value on 1 to 1024 neighbouring positions
- w_query: float32 [768, 768], P('dp', 'tensor'), may hold values from -0.21875 to 0.21875
- w_key: float32 [768, 768], P('dp', 'tensor'), may hold values from -0.21875 to 0.21875
- w_value: float32 [768, 768], P('dp', 'tensor'), may hold values from -0.21875 to 0.21875
- b_query: float32 [768], P('tensor'), may hold values from -3 to 3
- b_value: float32 [768], P('tensor'), may hold values from -3 to 3
- w_out: float32 [768, 768], P('tensor', 'dp'), may hold values from -0.875 to 0.875
- b_out: float32 [768], replicated, may hold values from -1.75 to 1.75
- gain_one: float32 [768], replicated, may hold values from 0.5 to 1.5
- shift_one: float32 [768], replicated, may hold values from -1.75 to 1.75
- w_up: float32 [768, 3072], P('dp', 'tensor'), may hold values from -0.21875 to 0.21875
- b_up: float32 [3072], P('tensor'), may hold values from -1.75 to 1.75
- w_down: float32 [3072, 768], P('tensor', 'dp'), may hold values from -0.109375 to 0.109375
- b_down: float32 [768], replicated, may hold values from -1.75 to 1.75
- gain_two: float32 [768], replicated, may hold values from 0.5 to 1.5
- shift_two: float32 [768], replicated, may hold values from -1.75 to 1.75
Outputs:
- layer_out: bfloat16 [12288, 768], P('dp')
- grad_tokens: bfloat16 [12288, 768], P('dp')
- query_grad: float32 [768, 768], P('dp', 'tensor')
- key_grad: float32 [768, 768], P('dp', 'tensor')
- value_grad: float32 [768, 768], P('dp', 'tensor')
- qbias_grad: float32 [768], P('tensor')
- vbias_grad: float32 [768], P('tensor')
- out_grad: float32 [768, 768], P('tensor', 'dp')
- obias_grad: float32 [768], replicated
- gain1_grad: float32 [768], replicated
- shift1_grad: float32 [768], replicated
- up_grad: float32 [768, 3072], P('dp', 'tensor')
- ubias_grad: float32 [3072], P('tensor')
- down_grad: float32 [3072, 768], P('tensor', 'dp')
- dbias_grad: float32 [768], replicated
- gain2_grad: float32 [768], replicated
- shift2_grad: float32 [768], replicated
Inputs may be any that keep to these rules, and one draw needn't show every extreme that they name: dealing is a permutation of the 12288 given-order tokens; the positions j*1536 to (j+1)*1536 - 1 form group j, and each group takes exactly 192 tokens from each block of 1536 given-order tokens. `segments`: row j gives the sequence of each position of group j: numbers never fall along a row, each sequence has 1 to 1024 positions, one has exactly 1024.
All inputs are finite; a program needn't handle non-finite values.
Results may differ from a plain program's by a relative error of at most 0.014.
The roundings to bfloat16 on the way count: a program that leaves them out, or rounds other values in their place, can miss the bound.
Values may be sent and summed in bfloat16 or wider, within the bound.
A program may use at most 128 MiB of HBM per device.

v0:
```python
import jax
import jax.numpy as jnp
from jax import lax
from jax.sharding import PartitionSpec as P

HEAD_DIM = 64


EPSILON = 1e-05
NEGATIVE = -1e30


def layer_norm(rows_in, gain, shift):
    center = rows_in - jnp.mean(rows_in, axis=-1, keepdims=True)
    spread = jnp.mean(center * center, axis=-1, keepdims=True)
    return center * lax.rsqrt(spread + EPSILON) * gain + shift


def norm_back(rows_in, gain, shift, upstream):
    result, pullback = jax.vjp(layer_norm, rows_in, gain, shift)
    return pullback(upstream)


def product(left, right):
    return jnp.dot(left, right, preferred_element_type=jnp.float32)


def exact_gelu(values):
    return jax.nn.gelu(values, approximate=False)


def tensor_total(partial_sum):
    return lax.psum(partial_sum, "tensor")


def shards(
    tokens,
    cotangent,
    dealing,
    segments,
    w_query,
    w_key,
    w_value,
    b_query,
    b_value,
    w_out,
    b_out,
    gain_one,
    shift_one,
    w_up,
    b_up,
    w_down,
    b_down,
    gain_two,
    shift_two,
):
    f32 = jnp.float32
    bf16 = jnp.bfloat16
    group_count = lax.axis_size("dp")
    row_count = tokens.shape[0]
    feat_width = tokens.shape[1]
    per_source = row_count // group_count
    heads_here = w_query.shape[1] // HEAD_DIM
    block_len = min(512, row_count)
    block_count = row_count // block_len
    source_dev = dealing // row_count
    source_row = dealing % row_count
    recv_order = jnp.argsort(source_dev, stable=True)
    placing = jnp.argsort(recv_order)
    request = source_row[recv_order].reshape(group_count, per_source)
    asked_rows = lax.all_to_all(request, "dp", split_axis=0, concat_axis=0, tiled=True).reshape(
        row_count
    )
    got_tokens, got_grads = (
        lax.all_to_all(
            tokens[asked_rows].reshape(group_count, per_source, feat_width),
            "dp",
            split_axis=0,
            concat_axis=0,
            tiled=True,
        ),
        lax.all_to_all(
            cotangent[asked_rows].reshape(group_count, per_source, feat_width),
            "dp",
            split_axis=0,
            concat_axis=0,
            tiled=True,
        ),
    )
    rows_in = got_tokens.reshape(row_count, feat_width)[placing]
    grad_out = got_grads.reshape(row_count, feat_width)[placing].astype(f32)
    residual = rows_in.astype(f32)
    seg_row = segments.reshape(row_count)
    query_w, key_w, value_w, out_w, up_w, down_w = (
        lax.all_gather(w_query.astype(bf16), "dp", axis=0, tiled=True),
        lax.all_gather(w_key.astype(bf16), "dp", axis=0, tiled=True),
        lax.all_gather(w_value.astype(bf16), "dp", axis=0, tiled=True),
        lax.all_gather(w_out.astype(bf16), "dp", axis=1, tiled=True),
        lax.all_gather(w_up.astype(bf16), "dp", axis=0, tiled=True),
        lax.all_gather(w_down.astype(bf16), "dp", axis=1, tiled=True),
    )
    queries = (
        ((product(rows_in, query_w) + b_query) * 0.125)
        .astype(bf16)
        .reshape(row_count, heads_here, HEAD_DIM)
    )
    key_rows = product(rows_in, key_w).astype(bf16).reshape(row_count, heads_here, HEAD_DIM)
    value_rows = (
        (product(rows_in, value_w) + b_value).astype(bf16).reshape(row_count, heads_here, HEAD_DIM)
    )

    def block_scores(block_idx):
        begin_row = block_idx * block_len
        query_blk = lax.dynamic_slice_in_dim(queries, begin_row, block_len, 0)
        seg_blk = lax.dynamic_slice_in_dim(seg_row, begin_row, block_len, 0)
        scores = jnp.einsum("qhd,khd->hqk", query_blk, key_rows, preferred_element_type=f32)
        same_doc = (seg_blk[:, None] == seg_row[None, :])[None]
        return (query_blk, jnp.where(same_doc, scores, NEGATIVE))

    def attend(block_idx):
        query_blk, scores = block_scores(block_idx)
        row_max = jnp.max(scores, axis=-1, keepdims=True)
        exp_scores = jnp.exp(scores - row_max)
        row_total = jnp.sum(exp_scores, axis=-1, keepdims=True)
        prob_low = (exp_scores / row_total).astype(bf16)
        mixed_blk = jnp.einsum("hqk,khd->qhd", prob_low, value_rows, preferred_element_type=f32)
        return (mixed_blk, (row_max + jnp.log(row_total))[..., 0])

    mixed_blocks, log_total = lax.map(attend, jnp.arange(block_count))
    mixed_low = mixed_blocks.reshape(row_count, heads_here * HEAD_DIM).astype(bf16)
    attn_part = product(mixed_low, out_w)
    first_in = residual + tensor_total(attn_part) + b_out
    first_norm = layer_norm(first_in, gain_one, shift_one)
    first_low = first_norm.astype(bf16)
    pre_act = product(first_low, up_w) + b_up
    hidden_low = exact_gelu(pre_act).astype(bf16)
    mlp_part = product(hidden_low, down_w)
    second_in = first_norm + tensor_total(mlp_part) + b_down
    result = layer_norm(second_in, gain_two, shift_two)
    grad_second, gain2_grad, shift2_grad = norm_back(second_in, gain_two, shift_two, grad_out)
    branch_low = grad_second.astype(bf16)
    dbias_grad = jnp.sum(branch_low, axis=0, dtype=f32)
    down_grad = jnp.einsum("rf,rd->fd", hidden_low, branch_low, preferred_element_type=f32)
    grad_hidden = jnp.einsum("rd,fd->rf", branch_low, down_w, preferred_element_type=f32)
    gelu_pull = jax.vjp(exact_gelu, pre_act)[1]
    grad_pre = gelu_pull(grad_hidden)[0].astype(bf16)
    ubias_grad = jnp.sum(grad_pre, axis=0, dtype=f32)
    up_grad = jnp.einsum("rd,rf->df", first_low, grad_pre, preferred_element_type=f32)
    back_part = jnp.einsum("rf,df->rd", grad_pre, up_w, preferred_element_type=f32)
    grad_first = grad_second + tensor_total(back_part)
    grad_attn_in, gain1_grad, shift1_grad = norm_back(first_in, gain_one, shift_one, grad_first)
    attn_low = grad_attn_in.astype(bf16)
    obias_grad = jnp.sum(attn_low, axis=0, dtype=f32)
    out_grad = jnp.einsum("rh,rd->hd", mixed_low, attn_low, preferred_element_type=f32)
    grad_mixed = (
        jnp.einsum("rd,hd->rh", attn_low, out_w, preferred_element_type=f32)
        .astype(bf16)
        .reshape(row_count, heads_here, HEAD_DIM)
    )

    def attend_back(running, block_idx):
        grad_keys, grad_values = running
        begin_row = block_idx * block_len
        query_blk, scores = block_scores(block_idx)
        grad_blk = lax.dynamic_slice_in_dim(grad_mixed, begin_row, block_len, 0)
        probs = jnp.exp(scores - log_total[block_idx][..., None])
        prob_low = probs.astype(bf16)
        grad_probs = jnp.einsum("qhd,khd->hqk", grad_blk, value_rows, preferred_element_type=f32)
        row_inner = jnp.sum(grad_probs * probs, axis=-1, keepdims=True)
        grad_scores = (probs * (grad_probs - row_inner)).astype(bf16)
        grad_query = jnp.einsum("hqk,khd->qhd", grad_scores, key_rows, preferred_element_type=f32)
        grad_keys = grad_keys + jnp.einsum(
            "hqk,qhd->khd", grad_scores, query_blk, preferred_element_type=f32
        )
        grad_values = grad_values + jnp.einsum(
            "hqk,qhd->khd", prob_low, grad_blk, preferred_element_type=f32
        )
        return ((grad_keys, grad_values), grad_query)

    empty_grad = jnp.zeros((row_count, heads_here, HEAD_DIM), f32)
    (grad_keys, grad_values), grad_query = lax.scan(
        attend_back, (empty_grad, empty_grad), jnp.arange(block_count)
    )
    grad_qpre = grad_query.reshape(row_count, heads_here * HEAD_DIM).astype(bf16) * 0.125
    keys_low = grad_keys.reshape(row_count, heads_here * HEAD_DIM).astype(bf16)
    values_low = grad_values.reshape(row_count, heads_here * HEAD_DIM).astype(bf16)
    qbias_grad = jnp.sum(grad_qpre, axis=0, dtype=f32)
    vbias_grad = jnp.sum(values_low, axis=0, dtype=f32)
    query_grad = jnp.einsum("rd,rh->dh", rows_in, grad_qpre, preferred_element_type=f32)
    key_grad = jnp.einsum("rd,rh->dh", rows_in, keys_low, preferred_element_type=f32)
    value_grad = jnp.einsum("rd,rh->dh", rows_in, values_low, preferred_element_type=f32)
    query_grad, key_grad, value_grad, out_grad, up_grad, down_grad = (
        lax.psum_scatter(query_grad, "dp", scatter_dimension=0, tiled=True),
        lax.psum_scatter(key_grad, "dp", scatter_dimension=0, tiled=True),
        lax.psum_scatter(value_grad, "dp", scatter_dimension=0, tiled=True),
        lax.psum_scatter(out_grad, "dp", scatter_dimension=1, tiled=True),
        lax.psum_scatter(up_grad, "dp", scatter_dimension=0, tiled=True),
        lax.psum_scatter(down_grad, "dp", scatter_dimension=1, tiled=True),
    )
    back_in = jnp.einsum("rh,dh->rd", grad_qpre, query_w, preferred_element_type=f32)
    back_in = back_in + jnp.einsum("rh,dh->rd", keys_low, key_w, preferred_element_type=f32)
    back_in = back_in + jnp.einsum("rh,dh->rd", values_low, value_w, preferred_element_type=f32)
    grad_in = grad_attn_in + tensor_total(back_in)
    (
        qbias_grad,
        vbias_grad,
        obias_grad,
        gain1_grad,
        shift1_grad,
        ubias_grad,
        dbias_grad,
        gain2_grad,
        shift2_grad,
    ) = lax.psum(
        (
            qbias_grad,
            vbias_grad,
            obias_grad,
            gain1_grad,
            shift1_grad,
            ubias_grad,
            dbias_grad,
            gain2_grad,
            shift2_grad,
        ),
        "dp",
    )
    out_low = result.astype(bf16)
    back_low = grad_in.astype(bf16)
    out_rows, grad_rows = (
        lax.all_to_all(
            out_low[recv_order].reshape(group_count, per_source, feat_width),
            "dp",
            split_axis=0,
            concat_axis=0,
            tiled=True,
        ),
        lax.all_to_all(
            back_low[recv_order].reshape(group_count, per_source, feat_width),
            "dp",
            split_axis=0,
            concat_axis=0,
            tiled=True,
        ),
    )
    restore = jnp.argsort(asked_rows)
    layer_out = out_rows.reshape(row_count, feat_width)[restore]
    grad_tokens = grad_rows.reshape(row_count, feat_width)[restore]
    return (
        layer_out,
        grad_tokens,
        query_grad,
        key_grad,
        value_grad,
        qbias_grad,
        vbias_grad,
        out_grad,
        obias_grad,
        gain1_grad,
        shift1_grad,
        up_grad,
        ubias_grad,
        down_grad,
        dbias_grad,
        gain2_grad,
        shift2_grad,
    )


def solution(mesh):
    in_specs = (
        P("dp", None),
        P("dp", None),
        P("dp"),
        P("dp", None),
        P("dp", "tensor"),
        P("dp", "tensor"),
        P("dp", "tensor"),
        P("tensor"),
        P("tensor"),
        P("tensor", "dp"),
        P(),
        P(),
        P(),
        P("dp", "tensor"),
        P("tensor"),
        P("tensor", "dp"),
        P(),
        P(),
        P(),
    )
    out_specs = (
        P("dp", None),
        P("dp", None),
        P("dp", "tensor"),
        P("dp", "tensor"),
        P("dp", "tensor"),
        P("tensor"),
        P("tensor"),
        P("tensor", "dp"),
        P(),
        P(),
        P(),
        P("dp", "tensor"),
        P("tensor"),
        P("tensor", "dp"),
        P(),
        P(),
        P(),
    )
    return jax.shard_map(shards, mesh=mesh, in_specs=in_specs, out_specs=out_specs, check_vma=False)
```

profile of v0, /device:TPU:0, one launch (start us, length us, event | category | flops | bytes accessed | tf_op | source)
XLA Modules:
  0.0 1102.2 jit_solution(10003411565259264094)
XLA Ops:
  14.0 8.4 gather_fusion
  22.4 9.7 all_to_all.29
  48.2 28.2 %all_gather.21 = bf16[192,768]{0,1:T(8,128)(2,1)} all-gather(bf16[192,96]{0,1:T(8,128)(2,1)S(1)} %copy.39), channel_id=1, replica_groups=mesh['dp'=8,'tensor'=4] {'dp'}, dimensions={1}, use_global_device_ids=true | all-gather | bytes 331776 | tf_op jit(solution)/shard_map/all_gather | solution.py:98
  76.4 9.6 all_gather.20
  86.0 9.5 all_gather.19
  95.5 9.9 all_gather.18
  119.2 38.2 %while.27 = (s32[]{:T(128)}, bf16[3,512,3,64]{1,3,2,0:T(8,128)(2,1)}, f32[3,3,512]{2,1,0:T(4,128)}, s32[3]{0:T(128)S(1)}, s32[1536]{0:T(1024)}, /*index=5*/s32[1...) while((s32[]{:T(128)}, ...), condition=%wide.region_5.6_spmd, body=%wide.region_2.5_spmd.sunk | while | flops 625998336 | bytes 38025632 | solution.py:129
  168.0 168.4 %all-reduce.6.cloned.1.call-done = f32[1536,768]{1,0:T(8,128)} async-done(((f32[1536,768]{1,0:T(8,128)}), f32[1536,768]{1,0:T(8,128)}) %all-reduce.6.cloned.1.call-update) | async-done | bytes 4718608 | tf_op jit(solution)/shard_map/psum | solution.py:33
  343.2 14.8 %multiply_convert_fusion.1 = (bf16[1536,768]{1,0:T(8,128)(2,1)}, f32[1536,768]{1,0:T(8,128)}, f32[1536,768]{1,0:T(8,128)}) fusion(f32[768]{0:T(1024)} %param.37, bf16[1536,768]{1,0:T(8,128)(2,1)S(1)} %fusion.43, bf16[768,768]{1,0:T(8,128)(2,1)} %all-gather.3.cloned.1.call-done), kind=kOutput, calls=%fused_computation.71 | convolution fusion | flops 1889796096 | bytes 15338496 | tf_op jit(solution)/shard_map/dot_general | solution.py:25
  358.0 6.2 fusion.57
  365.8 5.7 gather_fusion.5
  371.6 33.2 %all_to_all.30 = bf16[8,192,768]{2,1,0:T(8,128)(2,1)S(1)} all-to-all(bf16[8,192,768]{2,1,0:T(8,128)(2,1)} %bitcast.135), channel_id=1, replica_groups=mesh['dp'=8,'tensor'=4] {'dp'}, dimensions={0} | all-to-all | bytes 4718592 | tf_op jit(solution)/shard_map/all_to_all | solution.py:82
  404.8 5.7 gather_fusion.6
  410.5 124.8 %all-reduce.8.cloned.1.call-done = f32[1536,768]{1,0:T(8,128)} async-done(((f32[1536,768]{1,0:T(8,128)}), f32[1536,768]{1,0:T(8,128)}) %all-reduce.8.cloned.1.call-update) | async-done | bytes 4718608 | tf_op jit(solution)/shard_map/psum | solution.py:33
  563.3 171.0 %all-reduce.10.cloned.1.call-done = f32[1536,768]{1,0:T(8,128)} async-done(((f32[1536,768]{1,0:T(8,128)}), f32[1536,768]{1,0:T(8,128)}) %all-reduce.10.cloned.1.call-update) | async-done | bytes 4718608 | tf_op jit(solution)/shard_map/psum | solution.py:33
  734.3 8.0 multiply_reduce_fusion.1
  753.9 69.0 %while.28 = (s32[]{:T(128)}, f32[1536,3,64]{0,2,1:T(8,128)S(1)}, f32[1536,3,64]{0,2,1:T(8,128)S(1)}, bf16[3,512,3,64]{1,3,2,0:T(8,128)(2,1)}, s32[3]{0:T(128)}, ...) while((s32[]{:T(128)}, f32[1536,3,64]{0,2,1:T(8,128)S(1)}, ...), condition=%wide.region_20.21_spmd.clone, body=%wide.region_18.20_spmd.clone.sunk | while | flops 1540225536 | bytes 88791480 | solution.py:181
  834.9 6.6 fusion.65
  841.6 6.1 fusion.64
  859.8 142.4 %all-reduce.12.cloned.1.call-done = f32[1536,768]{1,0:T(8,128)} async-done(((f32[1536,768]{1,0:T(8,128)}), f32[1536,768]{1,0:T(8,128)}) %all-reduce.12.cloned.1.call-update) | async-done | bytes 4718608 | tf_op jit(solution)/shard_map/psum | solution.py:33
  1025.9 8.7 gather_fusion.4
  1034.8 31.1 %all-reduce = (f32[192]{0:T(256)}, f32[192]{0:T(256)}, f32[768]{0:T(1024)}, f32[768]{0:T(1024)}, f32[768]{0:T(1024)}, /*index=5*/f32[768]{0:T(1024)}, f32[768]{0:T(1024)}, f32[768]{0:T(1024)}, f32[768]{0:T(1024)}) all-reduce(f32[192]{0:T(256)S(1)} %reduce_sum.190, ...), channel_id=1, replica_groups=mesh['dp'=8,'tensor'=4] {'dp'}, use_global_device_ids=true, to_apply=%region_26.27 | all-reduce | flops 5760 | bytes 46080 | tf_op jit(solution)/shard_map/psum | solution.py:214
  1067.6 8.9 gather_fusion.8
  1076.5 18.4 %reduce-scatter.9.cloned.1.call-done = f32[96,192]{1,0:T(8,128)} async-done(((f32[768,192]{1,0:T(8,128)}), f32[96,192]{1,0:T(8,128)}) %reduce-scatter.9.cloned.1.call-update) | async-done | bytes 73744 | tf_op jit(solution)/shard_map/reduce_scatter | solution.py:193
  (368 shorter events, 239.6 us)
Async XLA Ops:
  8.0 24.8 %copy-start = (bf16[1536,768]{1,0:T(8,128)(2,1)S(1)}, bf16[1536,768]{1,0:T(8,128)(2,1)}, u32[]{:S(2)}) copy-start(bf16[1536,768]{1,0:T(8,128)(2,1)} %param.23) | copy-start | bytes 7077892
  14.0 24.5 %copy-start.37 = (s32[2048]{0:T(1024)}, s32[2048]{0:T(1024)S(1)}, u32[]{:S(2)}) copy-start(s32[2048]{0:T(1024)S(1)} %pad_clamp_fusion.3) | copy-start | bytes 24580
  38.5 9.6 copy-start.41
  38.5 9.6 copy-start.42
  38.5 67.0 %all-to-all-start.1 = ((bf16[8,192,768]{2,1,0:T(8,128)(2,1)}), bf16[8,192,768]{2,1,0:T(8,128)(2,1)S(1)}, u32[]{:S(2)}, u32[]{:S(2)}) async-start(bf16[8,192,768]{2,1,0:T(8,128)(2,1)} %bitcast.133), calls=%async_computation.1 | async-start | bytes 4718592 | tf_op jit(solution)/shard_map/all_to_all | solution.py:75
  42.3 294.1 %all-reduce.6.cloned.1.call-start = ((), (), s32[]{:S(2)}) async-start(), calls=%async_computation.11 | async-start | bytes 9437184 | tf_op jit(solution)/shard_map/psum | solution.py:33
  95.5 15.6 %copy-start.14 = (bf16[768,192]{1,0:T(8,128)(2,1)}, bf16[768,192]{1,0:T(8,128)(2,1)S(1)}, u32[]{:S(2)}) copy-start(bf16[768,192]{1,0:T(8,128)(2,1)S(1)} %all_gather.19) | copy-start | bytes 884740
  159.9 176.4 %copy-start.64 = (f32[768]{0:T(1024)S(1)}, f32[768]{0:T(1024)}, u32[]{:S(2)}) copy-start(f32[768]{0:T(1024)} %param.33) | copy-start | bytes 9220
  164.0 179.2 %all-gather.3.cloned.1.call-start = ((), (), s32[]{:S(2)}) async-start(), calls=%async_computation.12 | async-start | bytes 1327104 | tf_op jit(solution)/shard_map/all_gather | solution.py:99
  165.7 192.3 %all-gather.5.cloned.1.call-start = ((), (), s32[]{:S(2)}) async-start(), calls=%async_computation.13 | async-start | bytes 1327104 | tf_op jit(solution)/shard_map/all_gather | solution.py:100
  167.4 367.9 %all-reduce.8.cloned.1.call-start = ((), (), s32[]{:S(2)}) async-start(), calls=%async_computation.14 | async-start | bytes 9437184 | tf_op jit(solution)/shard_map/psum | solution.py:33
  343.2 14.8 %copy-start.11 = (bf16[1536,768]{1,0:T(8,128)(2,1)}, bf16[1536,768]{1,0:T(8,128)(2,1)S(1)}, u32[]{:S(2)}) copy-start(bf16[1536,768]{1,0:T(8,128)(2,1)S(1)} %fusion.43) | copy-start | bytes 7077892
  364.2 370.1 %all-reduce.10.cloned.1.call-start = ((), (), s32[]{:S(2)}) async-start(), calls=%async_computation.15 | async-start | bytes 9437184 | tf_op jit(solution)/shard_map/psum | solution.py:33
  563.2 439.1 %all-reduce.12.cloned.1.call-start = ((), (), s32[]{:S(2)}) async-start(), calls=%async_computation.16 | async-start | bytes 9437184 | tf_op jit(solution)/shard_map/psum | solution.py:33
  831.2 234.8 %reduce-scatter.19.cloned.1.call-start = ((), (), s32[]{:S(2)}) async-start(), calls=%async_computation.22 | async-start | bytes 884736
  834.9 241.6 %reduce-scatter.17.cloned.1.call-start = ((), (), s32[]{:S(2)}) async-start(), calls=%async_computation.21 | async-start | bytes 2654208 | tf_op jit(solution)/shard_map/reduce_scatter | solution.py:198
  841.6 234.9 %reduce-scatter.15.cloned.1.call-start = ((), (), s32[]{:S(2)}) async-start(), calls=%async_computation.20 | async-start | bytes 2654208 | tf_op jit(solution)/shard_map/reduce_scatter | solution.py:197
  853.4 148.9 %copy-start.51 = (f32[1536]{0:T(1024)S(1)}, f32[1536]{0:T(1024)}, u32[]{:S(2)}) copy-start(f32[1536]{0:T(1024)} %copy-done.50) | copy-start | bytes 18436
  853.4 158.8 %all-to-all-start.2 = ((bf16[8,192,768]{2,1,0:T(8,128)(2,1)}), bf16[8,192,768]{2,1,0:T(8,128)(2,1)}, u32[]{:S(2)}, u32[]{:S(2)}) async-start(bf16[8,192,768]{2,1,0:T(8,128)(2,1)} %bitcast.134), calls=%async_computation.2 | async-start | bytes 4718592 | tf_op jit(solution)/shard_map/all_to_all | solution.py:231
  858.0 218.4 %reduce-scatter.13.cloned.1.call-start = ((), (), s32[]{:S(2)}) async-start(), calls=%async_computation.19 | async-start | bytes 884736 | tf_op jit(solution)/shard_map/reduce_scatter | solution.py:195
  1012.2 55.4 %all-to-all-start.4 = ((bf16[8,192,768]{2,1,0:T(8,128)(2,1)}), bf16[8,192,768]{2,1,0:T(8,128)(2,1)}, u32[]{:S(2)}, u32[]{:S(2)}) async-start(bf16[8,192,768]{2,1,0:T(8,128)(2,1)} %bitcast.132), calls=%async_computation.4 | async-start | bytes 4718592 | tf_op jit(solution)/shard_map/all_to_all | solution.py:238
  1016.9 59.6 %reduce-scatter.11.cloned.1.call-start = ((), (), s32[]{:S(2)}) async-start(), calls=%async_computation.18 | async-start | bytes 884736 | tf_op jit(solution)/shard_map/reduce_scatter | solution.py:194
  1018.9 76.0 %reduce-scatter.9.cloned.1.call-start = ((), (), s32[]{:S(2)}) async-start(), calls=%async_computation.17 | async-start | bytes 884736 | tf_op jit(solution)/shard_map/reduce_scatter | solution.py:193
  1067.6 27.3 %copy-start.1 = (bf16[1536,768]{1,0:T(8,128)(2,1)S(1)}, bf16[1536,768]{1,0:T(8,128)(2,1)}, u32[]{:S(2)}) copy-start(bf16[1536,768]{1,0:T(8,128)(2,1)} %param.23) | copy-start | bytes 7077892
  (87 other events, 374.1 us)
Sparse Core Ops, SparseCore 0:
  164.1 172.2 all-reduce.5
  364.3 170.9 all-reduce.7
  563.3 170.9 all-reduce.9
  831.3 170.9 all-reduce.11
Sparse Core Ops, SparseCore 1:
  166.9 24.0 all-gather.2
  193.3 23.8 all-gather.4
  835.0 34.8 reduce-scatter.18
  873.7 46.3 reduce-scatter.16
  924.0 42.2 reduce-scatter.14
  970.0 34.9 reduce-scatter.12
  1021.1 35.1 reduce-scatter.10
  1059.9 34.9 reduce-scatter.8
where the time goes:
time: 1110 us; the launch traced here: 1100 us
  waiting for transfers between devices  625 us (56%)
  blocking collectives  131 us (12%)
  matrix products  120 us (11%)
  local copies, waits for them, and re-layouts  95.6 us (9%)
  other arithmetic  88.9 us (8%)
  between operations  16.4 us (1%)
  starting transfers between devices  14.3 us (1%)
    psum x4, waiting for transfers between devices, tensor_total(): return lax.psum(partial_sum, 'tensor')  607 us
    all_to_all x1, blocking collectives, shards(): lax.all_to_all(cotangent[asked_rows].reshape(group_count, per_source, fea...  33.2 us
    dot_general x6, matrix products, product(): return jnp.dot(left, right, preferred_element_type=jnp.float32)  32.2 us
    psum x1, blocking collectives, shards(): lax.psum((qbias_grad, vbias_grad, obias_grad, gain1_grad, shift1_grad, ub...  31.1 us
    all_gather x1, blocking collectives, shards(): lax.all_gather(w_out.astype(bf16), 'dp', axis=1, tiled=True)  28.2 us
  transfers between devices with their start and end apart: 15, of which 5 were waited for; matrix products, arithmetic and copies ran while one was open for 9% of the time, Pallas kernels for 0%

commit v1 on v0

v1 whole, which is shorter than its diff:
```python
import functools

import jax
import jax.numpy as jnp
from jax import lax
from jax.experimental import pallas as pl
from jax.experimental.pallas import tpu as pltpu
from jax.sharding import PartitionSpec as P

HEAD_DIM = 64
EPSILON = 1e-05
NEGATIVE = -1e30
MESH = pl.DeviceIdType.MESH
F32 = jnp.float32
BF16 = jnp.bfloat16
VMEM_LIMIT = 56 * 1024 * 1024


def vmem_spec():
    return pl.BlockSpec(memory_space=pltpu.VMEM)


def layer_norm(rows_in, gain, shift):
    center = rows_in - jnp.mean(rows_in, axis=-1, keepdims=True)
    spread = jnp.mean(center * center, axis=-1, keepdims=True)
    return center * lax.rsqrt(spread + EPSILON) * gain + shift


def norm_back(rows_in, gain, shift, upstream):
    result, pullback = jax.vjp(layer_norm, rows_in, gain, shift)
    return pullback(upstream)


def exact_gelu(values):
    return jax.nn.gelu(values, approximate=False)


def remote(src, dst, send_sem, recv_sem, device):
    return pltpu.make_async_remote_copy(
        src_ref=src,
        dst_ref=dst,
        send_sem=send_sem,
        recv_sem=recv_sem,
        device_id=device,
        device_id_type=MESH,
    )


def greet(devices):
    barrier = pltpu.get_barrier_semaphore()
    for device in devices:
        pl.semaphore_signal(barrier, inc=1, device_id=device, device_id_type=MESH)
    pl.semaphore_wait(barrier, len(devices))


def comm_call(kernel, out_shape, scratch, cid, args):
    return pl.pallas_call(
        kernel,
        out_shape=out_shape,
        in_specs=[vmem_spec()] * len(args),
        out_specs=[vmem_spec()] * len(out_shape),
        scratch_shapes=scratch,
        compiler_params=pltpu.CompilerParams(
            collective_id=cid, has_side_effects=True, vmem_limit_bytes=VMEM_LIMIT
        ),
    )(*args)


def meta_kernel(nd, nz, meta_ref, bias_ref, meta_out, bias_out, ssem, rsem):
    d, z = lax.axis_index("dp"), lax.axis_index("tensor")
    plane = [{"dp": lax.rem(d + k, nd)} for k in range(1, nd)]
    column = [{"tensor": lax.rem(z + k, nz)} for k in range(1, nz)]
    greet(plane + column)
    copies = []
    for i, device in enumerate(plane):
        copies.append(remote(meta_ref, meta_out.at[d], ssem.at[i], rsem.at[i], device))
    for j, device in enumerate(column):
        i = len(plane) + j
        copies.append(remote(bias_ref, bias_out.at[z], ssem.at[i], rsem.at[i], device))
    for copy in copies:
        copy.start()
    meta_out[d] = meta_ref[...]
    bias_out[z] = bias_ref[...]
    for copy in copies:
        copy.wait()


def index_kernel(nd, gpp, rows, meta_ref, loc_ref, seg_ref):
    per = rows // nd
    d, z = lax.axis_index("dp"), lax.axis_index("tensor")
    group = z * gpp + d // 4
    lane_i = lax.broadcasted_iota(jnp.int32, (128, 128), 0)
    lane_j = lax.broadcasted_iota(jnp.int32, (128, 128), 1)
    upper = (lane_i <= lane_j).astype(F32)
    row_i = lax.broadcasted_iota(jnp.int32, (16, 16), 0)
    row_j = lax.broadcasted_iota(jnp.int32, (16, 16), 1)
    lower = (row_j < row_i).astype(F32)
    rank_of = lax.broadcasted_iota(jnp.int32, (per, 128), 0).astype(F32)

    def pick(deal, source, values):
        low = source * rows
        hit = (deal >= low) & (deal < low + rows)
        ones = jnp.where(hit, 1.0, 0.0)
        inner = jnp.dot(ones, upper, preferred_element_type=F32)
        total = jnp.broadcast_to(inner[:, 127:128], (16, 128))
        before = jnp.dot(lower, total, preferred_element_type=F32)
        key = jnp.where(hit, inner + before - 1.0, -1.0)
        found = jnp.zeros((per, 128), F32)
        for c in range(rows // 128):
            found = found + jnp.where(rank_of == key[c : c + 1, :], values[c : c + 1, :], 0.0)
        return jnp.sum(found, axis=1, keepdims=True).astype(jnp.int32)

    for g in range(nd):
        deal = meta_ref[g, 0:16, :]
        loc_ref[g] = pick(deal, d, (deal - d * rows).astype(F32))
    own_deal = meta_ref[group, 0:16, :]
    own_seg = meta_ref[group, 16:32, :].astype(F32)
    for s in range(nd):
        seg_ref[s] = pick(own_deal, s, own_seg)


def gather_kernel(nd, gpp, rows, loc_ref, tok_ref, cot_ref, tok_out, cot_out):
    per = rows // nd
    z = lax.axis_index("tensor")
    column = lax.broadcasted_iota(jnp.int32, (per, rows), 1)
    for k in range(gpp):
        loc = loc_ref[z * gpp + k]
        pick = jnp.where(column == loc, 1.0, 0.0).astype(BF16)
        tok_out[k] = jnp.dot(pick, tok_ref[...], preferred_element_type=F32).astype(BF16)
        cot_out[k] = jnp.dot(pick, cot_ref[...], preferred_element_type=F32).astype(BF16)


def dispatch_kernel(
    nd, nz, gpp, tok_ref, cot_ref, wqkv_ref, x_out, cot_out, w_out, ssem, rsem, lsem
):
    d, z = lax.axis_index("dp"), lax.axis_index("tensor")
    t = lax.rem(d, 4)
    quarter = nd // 4
    everyone = []
    for kz in range(nz):
        for kd in range(nd):
            if kz or kd:
                everyone.append({"dp": lax.rem(d + kd, nd), "tensor": lax.rem(z + kz, nz)})
    greet(everyone)
    waits = []
    locals_ = []
    for k in range(1, nd):
        dest = lax.rem(d + k, nd)
        copy = remote(tok_ref.at[dest // 4], x_out.at[d], ssem.at[k], rsem.at[k], {"dp": dest})
        copy.start()
        waits.append(copy)
    own = pltpu.make_async_copy(tok_ref.at[d // 4], x_out.at[d], lsem.at[0])
    own.start()
    locals_.append(own)
    base = nd
    for m in range(gpp):
        for kz in range(nz):
            dest = 4 * m + z
            dz = lax.rem(z + kz, nz)
            copy = remote(
                wqkv_ref,
                w_out.at[d],
                ssem.at[base + m * nz + kz],
                rsem.at[base + d],
                {"dp": dest, "tensor": dz},
            )
            if kz == 0:

                @pl.when(dest != d)
                def _():
                    copy.start()

                @pl.when(dest == d)
                def _():
                    pltpu.make_async_copy(wqkv_ref, w_out.at[d], lsem.at[1]).start()
            else:
                copy.start()
    base_c = base + max(nd, gpp * nz)
    for k in range(gpp):
        dest = 4 * k + d // quarter
        copy = remote(
            cot_ref.at[k],
            cot_out.at[lax.rem(d, quarter)],
            ssem.at[base_c + k],
            rsem.at[base_c + lax.rem(d, quarter)],
            {"dp": dest},
        )

        @pl.when(dest != d)
        def _():
            copy.start()

        @pl.when(dest == d)
        def _():
            pltpu.make_async_copy(
                cot_ref.at[k], cot_out.at[lax.rem(d, quarter)], lsem.at[2]
            ).start()

    for copy in waits:
        copy.wait()
    for copy in locals_:
        copy.wait()
    for m in range(gpp):
        for kz in range(nz):
            dest = 4 * m + z
            send = remote(
                wqkv_ref,
                w_out.at[d],
                ssem.at[base + m * nz + kz],
                rsem.at[base + d],
                {"dp": dest, "tensor": lax.rem(z + kz, nz)},
            )
            if kz == 0:

                @pl.when(dest != d)
                def _():
                    send.wait_send()

                @pl.when(dest == d)
                def _():
                    pltpu.make_async_copy(wqkv_ref, w_out.at[d], lsem.at[1]).wait()
            else:
                send.wait_send()
    for s in range(nd):
        came = remote(
            wqkv_ref, w_out.at[s], ssem.at[base], rsem.at[base + s], {"dp": s, "tensor": t}
        )

        @pl.when(jnp.logical_or(t != z, d != s))
        def _():
            came.wait_recv()

    for k in range(gpp):
        dest = 4 * k + d // quarter
        send = remote(
            cot_ref.at[k],
            cot_out.at[lax.rem(d, quarter)],
            ssem.at[base_c + k],
            rsem.at[base_c + lax.rem(d, quarter)],
            {"dp": dest},
        )

        @pl.when(dest != d)
        def _():
            send.wait_send()

        @pl.when(dest == d)
        def _():
            pltpu.make_async_copy(
                cot_ref.at[k], cot_out.at[lax.rem(d, quarter)], lsem.at[2]
            ).wait()

    for j in range(quarter):
        source = t * quarter + j
        came = remote(
            cot_ref.at[0], cot_out.at[j], ssem.at[base_c], rsem.at[base_c + j], {"dp": source}
        )

        @pl.when(source != d)
        def _():
            came.wait_recv()


def quad_kernel(nd, in_ref, out_ref, ssem, rsem):
    d = lax.axis_index("dp")
    t = lax.rem(d, 4)
    first = d - t
    peers = [lax.rem(t + k, 4) for k in range(1, 4)]
    greet([{"dp": first + peer} for peer in peers])
    copies = []
    for i, peer in enumerate(peers):
        copies.append(
            remote(in_ref.at[peer], out_ref.at[t], ssem.at[i], rsem.at[i], {"dp": first + peer})
        )
    for copy in copies:
        copy.start()
    out_ref[t] = in_ref[t]
    for copy in copies:
        copy.wait()


def back_kernel(
    nd, nz, gpp, part_ref, vec_ref, dw_ref, part_out, vec_out, dw_out, ssem, rsem, lsem
):
    d, z = lax.axis_index("dp"), lax.axis_index("tensor")
    t = lax.rem(d, 4)
    first = d - t
    everyone = []
    for kz in range(nz):
        for kd in range(nd):
            if kz or kd:
                everyone.append({"dp": lax.rem(d + kd, nd), "tensor": lax.rem(z + kz, nz)})
    greet(everyone)
    copies = []
    for k in range(1, 4):
        peer = lax.rem(t + k, 4)
        copies.append(
            remote(part_ref.at[peer], part_out.at[t], ssem.at[k], rsem.at[k], {"dp": first + peer})
        )
    for k in range(1, nd):
        copies.append(
            remote(vec_ref, vec_out.at[d], ssem.at[3 + k], rsem.at[3 + k], {"dp": lax.rem(d + k, nd)})
        )
    for copy in copies:
        copy.start()
    base = 3 + nd
    slot = z * gpp + d // 4

    def send_dw(k):
        dest = lax.rem(d + k, nd)
        return remote(
            dw_ref.at[dest],
            dw_out.at[slot],
            ssem.at[base + k],
            rsem.at[base + slot],
            {"dp": dest, "tensor": t},
        )

    own = pltpu.make_async_copy(dw_ref.at[d], dw_out.at[slot], lsem.at[0])
    for k in range(nd):
        if k == 0:

            @pl.when(t != z)
            def _():
                send_dw(0).start()

            @pl.when(t == z)
            def _():
                own.start()
        else:
            send_dw(k).start()
    part_out[t] = part_ref[t]
    vec_out[d] = vec_ref[...]
    for copy in copies:
        copy.wait()
    for k in range(nd):
        if k == 0:

            @pl.when(t != z)
            def _():
                send_dw(0).wait_send()

            @pl.when(t == z)
            def _():
                own.wait()
        else:
            send_dw(k).wait_send()
    for sz in range(nz):
        for k in range(gpp):
            source = 4 * k + z
            came = remote(
                dw_ref.at[0],
                dw_out.at[sz * gpp + k],
                ssem.at[base],
                rsem.at[base + sz * gpp + k],
                {"dp": source, "tensor": sz},
            )

            @pl.when(jnp.logical_or(source != d, z != sz))
            def _():
                came.wait_recv()


def combine_kernel(nd, nz, gpp, count, *refs):
    row_refs, (vec_ref,) = refs[:count], refs[count : count + 1]
    outs, (vec_out,) = refs[count + 1 : 2 * count + 1], refs[2 * count + 1 : 2 * count + 2]
    ssem, rsem, usend, urecv, dsend, drecv, vsend, vrecv, lsem = refs[2 * count + 2 :]
    d, z = lax.axis_index("dp"), lax.axis_index("tensor")
    t = lax.rem(d, 4)
    quarter = nd // 4
    plane = [{"dp": lax.rem(d + k, nd)} for k in range(1, nd)]
    column = [{"tensor": lax.rem(z + k, nz)} for k in range(1, nz)]
    greet(plane + column)
    vecs = []
    for k in range(1, nz):
        copy = remote(vec_ref, vec_out.at[z], vsend.at[k], vrecv.at[k], {"tensor": lax.rem(z + k, nz)})
        copy.start()
        vecs.append(copy)
    vec_out[z] = vec_ref[...]
    for i in range(count):
        for b in range(quarter):
            dest = t * quarter + b
            copy = remote(
                row_refs[i].at[b],
                outs[i].at[z, d // 4],
                ssem.at[i, b],
                rsem.at[i, d // 4],
                {"dp": dest},
            )
            own = pltpu.make_async_copy(row_refs[i].at[b], outs[i].at[z, d // 4], lsem.at[i])

            @pl.when(dest != d)
            def _():
                copy.start()

            @pl.when(dest == d)
            def _():
                own.start()

    def hop(i, k, up):
        block = z - k if up else z + k
        block = jnp.clip(block, 0, nz - 1)
        peer = jnp.clip(z + 1 if up else z - 1, 0, nz - 1)
        sems = (usend, urecv) if up else (dsend, drecv)
        return remote(
            outs[i].at[block], outs[i].at[block], sems[0].at[i, k], sems[1].at[i, k], {"tensor": peer}
        )

    def sends(k, up):
        return (z - k >= 0) & (z + 1 < nz) if up else (z + k < nz) & (z - 1 >= 0)

    def gets(k, up):
        return z - 1 - k >= 0 if up else z + 1 + k < nz

    def came(i, k, up):
        block = jnp.clip(z - 1 - k if up else z + 1 + k, 0, nz - 1)
        peer = jnp.clip(z - 1 if up else z + 1, 0, nz - 1)
        sems = (usend, urecv) if up else (dsend, drecv)
        return remote(
            outs[i].at[block], outs[i].at[block], sems[0].at[i, k], sems[1].at[i, k], {"tensor": peer}
        )

    for i in range(count):
        for k in range(gpp):
            source = 4 * k + d // quarter
            arrive = remote(
                row_refs[i].at[0], outs[i].at[z, k], ssem.at[i, 0], rsem.at[i, k], {"dp": source}
            )

            @pl.when(source != d)
            def _():
                arrive.wait_recv()

            @pl.when(source == d)
            def _():
                pltpu.make_async_copy(row_refs[i].at[0], outs[i].at[z, k], lsem.at[i]).wait()

        for up in (True, False):

            @pl.when(sends(0, up))
            def _():
                hop(i, 0, up).start()

    for k in range(nz - 1):
        for i in range(count):
            for up in (True, False):

                @pl.when(gets(k, up))
                def _():
                    came(i, k, up).wait_recv()

                if k + 1 < nz - 1:

                    @pl.when(sends(k + 1, up))
                    def _():
                        hop(i, k + 1, up).start()

    for k in range(nz - 1):
        for i in range(count):
            for up in (True, False):

                @pl.when(sends(k, up))
                def _():
                    hop(i, k, up).wait_send()

    for i in range(count):
        for b in range(quarter):
            dest = t * quarter + b
            copy = remote(
                row_refs[i].at[b],
                outs[i].at[z, d // 4],
                ssem.at[i, b],
                rsem.at[i, d // 4],
                {"dp": dest},
            )

            @pl.when(dest != d)
            def _():
                copy.wait_send()

    for copy in vecs:
        copy.wait()


def attend_kernel(heads, q_ref, kv_ref, segc_ref, segr_ref, mix_ref, lse_ref):
    width = heads * HEAD_DIM
    same = segc_ref[...] == segr_ref[...]
    lane = lax.broadcasted_iota(jnp.int32, lse_ref.shape, 1)
    lse_all = jnp.zeros(lse_ref.shape, F32)
    mixes = []
    for h in range(heads):
        cut = slice(h * HEAD_DIM, (h + 1) * HEAD_DIM)
        query = q_ref[:, cut]
        keys = kv_ref[:, width + h * HEAD_DIM : width + (h + 1) * HEAD_DIM]
        values = kv_ref[:, 2 * width + h * HEAD_DIM : 2 * width + (h + 1) * HEAD_DIM]
        scores = lax.dot_general(query, keys, (((1,), (1,)), ((), ())), preferred_element_type=F32)
        scores = jnp.where(same, scores, NEGATIVE)
        top = jnp.max(scores, axis=1, keepdims=True)
        powers = jnp.exp(scores - top)
        total = jnp.sum(powers, axis=1, keepdims=True)
        prob_low = (powers * (1.0 / total)).astype(BF16)
        mixes.append(jnp.dot(prob_low, values, preferred_element_type=F32).astype(BF16))
        lse_all = jnp.where(lane == h, top + jnp.log(total), lse_all)
    mix_ref[...] = jnp.concatenate(mixes, axis=1)
    lse_ref[...] = lse_all


def attend(qkv, seg_col, seg_row, heads, block):
    rows = qkv.shape[0]
    return pl.pallas_call(
        functools.partial(attend_kernel, heads),
        grid=(rows // block,),
        in_specs=[
            pl.BlockSpec((block, qkv.shape[1]), lambda i: (i, 0)),
            pl.BlockSpec((rows, qkv.shape[1]), lambda i: (0, 0)),
            pl.BlockSpec((block, 1), lambda i: (i, 0)),
            pl.BlockSpec((1, rows), lambda i: (0, 0)),
        ],
        out_specs=[
            pl.BlockSpec((block, heads * HEAD_DIM), lambda i: (i, 0)),
            pl.BlockSpec((block, 128), lambda i: (i, 0)),
        ],
        out_shape=[
            jax.ShapeDtypeStruct((rows, heads * HEAD_DIM), BF16),
            jax.ShapeDtypeStruct((rows, 128), F32),
        ],
        compiler_params=pltpu.CompilerParams(vmem_limit_bytes=VMEM_LIMIT),
    )(qkv, qkv, seg_col, seg_row)


def attend_back_kernel(
    heads, steps, q_ref, kv_ref, g_ref, lse_ref, segc_ref, segr_ref, dq_ref, dkv_ref, dk_acc, dv_acc
):
    step = pl.program_id(0)
    width = heads * HEAD_DIM
    same = segc_ref[...] == segr_ref[...]
    dqs = []
    for h in range(heads):
        cut = slice(h * HEAD_DIM, (h + 1) * HEAD_DIM)
        query = q_ref[:, cut]
        keys = kv_ref[:, width + h * HEAD_DIM : width + (h + 1) * HEAD_DIM]
        values = kv_ref[:, 2 * width + h * HEAD_DIM : 2 * width + (h + 1) * HEAD_DIM]
        grad = g_ref[:, cut]
        scores = lax.dot_general(query, keys, (((1,), (1,)), ((), ())), preferred_element_type=F32)
        scores = jnp.where(same, scores, NEGATIVE)
        probs = jnp.exp(scores - lse_ref[:, h : h + 1])
        grad_probs = lax.dot_general(
            grad, values, (((1,), (1,)), ((), ())), preferred_element_type=F32
        )
        inner = jnp.sum(grad_probs * probs, axis=1, keepdims=True)
        grad_scores = (probs * (grad_probs - inner)).astype(BF16)
        prob_low = probs.astype(BF16)
        dqs.append(jnp.dot(grad_scores, keys, preferred_element_type=F32))
        dk = lax.dot_general(
            grad_scores, query, (((0,), (0,)), ((), ())), preferred_element_type=F32
        )
        dv = lax.dot_general(prob_low, grad, (((0,), (0,)), ((), ())), preferred_element_type=F32)

        @pl.when(step == 0)
        def _():
            dk_acc[h] = dk
            dv_acc[h] = dv

        @pl.when(step > 0)
        def _():
            dk_acc[h] += dk
            dv_acc[h] += dv

    dq_ref[...] = (jnp.concatenate(dqs, axis=1).astype(BF16) * 0.125).astype(BF16)

    @pl.when(step == steps - 1)
    def _():
        dkv_ref[:, :width] = jnp.concatenate([dk_acc[h] for h in range(heads)], axis=1).astype(BF16)
        dkv_ref[:, width:] = jnp.concatenate([dv_acc[h] for h in range(heads)], axis=1).astype(BF16)


def attend_back(qkv, grad, lse, seg_col, seg_row, heads, block):
    rows = qkv.shape[0]
    width = heads * HEAD_DIM
    steps = rows // block
    return pl.pallas_call(
        functools.partial(attend_back_kernel, heads, steps),
        grid=(steps,),
        in_specs=[
            pl.BlockSpec((block, qkv.shape[1]), lambda i: (i, 0)),
            pl.BlockSpec((rows, qkv.shape[1]), lambda i: (0, 0)),
            pl.BlockSpec((block, width), lambda i: (i, 0)),
            pl.BlockSpec((block, 128), lambda i: (i, 0)),
            pl.BlockSpec((block, 1), lambda i: (i, 0)),
            pl.BlockSpec((1, rows), lambda i: (0, 0)),
        ],
        out_specs=[
            pl.BlockSpec((block, width), lambda i: (i, 0)),
            pl.BlockSpec((rows, 2 * width), lambda i: (0, 0)),
        ],
        out_shape=[
            jax.ShapeDtypeStruct((rows, width), BF16),
            jax.ShapeDtypeStruct((rows, 2 * width), BF16),
        ],
        scratch_shapes=[
            pltpu.VMEM((heads, rows, HEAD_DIM), F32),
            pltpu.VMEM((heads, rows, HEAD_DIM), F32),
        ],
        compiler_params=pltpu.CompilerParams(vmem_limit_bytes=VMEM_LIMIT),
    )(qkv, qkv, grad, lse, seg_col, seg_row)


def restore_kernel(count, loc_ref, *refs):
    ins, outs = refs[:count], refs[count:]
    block = outs[0].shape[0]
    row = lax.broadcasted_iota(jnp.int32, (block, loc_ref.shape[1]), 0) + pl.program_id(0) * block
    pick = jnp.where(row == loc_ref[...], 1.0, 0.0).astype(BF16)
    for i in range(count):
        outs[i][...] = jnp.dot(pick, ins[i][...], preferred_element_type=F32).astype(BF16)


def restore(loc_row, arrays, block):
    rows, width = arrays[0].shape
    count = len(arrays)
    return pl.pallas_call(
        functools.partial(restore_kernel, count),
        grid=(rows // block,),
        in_specs=[pl.BlockSpec((1, rows), lambda i: (0, 0))]
        + [pl.BlockSpec((rows, width), lambda i: (0, 0))] * count,
        out_specs=[pl.BlockSpec((block, width), lambda i: (i, 0))] * count,
        out_shape=[jax.ShapeDtypeStruct((rows, width), BF16)] * count,
        compiler_params=pltpu.CompilerParams(vmem_limit_bytes=VMEM_LIMIT),
    )(loc_row, *arrays)


def shards(
    tokens,
    cotangent,
    dealing,
    segments,
    w_query,
    w_key,
    w_value,
    b_query,
    b_value,
    w_out,
    b_out,
    gain_one,
    shift_one,
    w_up,
    b_up,
    w_down,
    b_down,
    gain_two,
    shift_two,
):
    nd, nz = lax.axis_size("dp"), lax.axis_size("tensor")
    rows, width = tokens.shape
    gpp = nd // 4
    per = rows // nd
    part = rows // 4
    slab = w_query.shape[0]
    cols = w_query.shape[1]
    heads = cols // HEAD_DIM
    ff = w_up.shape[1]
    d, z = lax.axis_index("dp"), lax.axis_index("tensor")
    t = d % 4
    sds = jax.ShapeDtypeStruct
    dma = pltpu.SemaphoreType.DMA

    shard = jnp.concatenate([w_up, w_down.T, w_out.T], axis=1).astype(BF16)
    whole = lax.all_gather(shard, ("tensor", "dp"), axis=0, tiled=True)
    whole = whole.reshape(nz, width, 2 * ff + cols)
    up_w, down_t, out_t = whole[:, :, :ff], whole[:, :, ff : 2 * ff], whole[:, :, 2 * ff :]

    pad = 16 - rows // 128
    meta = jnp.concatenate(
        [
            jnp.pad(dealing.reshape(rows // 128, 128), ((0, pad), (0, 0)), constant_values=-1),
            jnp.pad(segments.reshape(rows // 128, 128), ((0, pad), (0, 0))),
        ]
    )
    bias = jnp.concatenate([b_query, b_value, b_up]).reshape(-1, 128)
    bias_rows = bias.shape[0]
    bias = jnp.pad(bias, ((0, -bias_rows % 8), (0, 0)))
    n_meta = nd - 1 + nz - 1
    meta_all, bias_all = comm_call(
        functools.partial(meta_kernel, nd, nz),
        [sds((nd, 32, 128), jnp.int32), sds((nz,) + bias.shape, F32)],
        [dma((n_meta,)), dma((n_meta,))],
        0,
        (meta, bias),
    )
    bias_all = bias_all[:, :bias_rows].reshape(nz, bias_rows * 128)
    own_bias = lax.dynamic_index_in_dim(bias_all, t, 0, keepdims=False)
    bq, bv = own_bias[:cols], own_bias[cols : 2 * cols]
    bu = bias_all[:, 2 * cols :]

    loc_all, seg_in = pl.pallas_call(
        functools.partial(index_kernel, nd, gpp, rows),
        in_specs=[vmem_spec()],
        out_specs=[vmem_spec()] * 2,
        out_shape=[sds((nd, per, 1), jnp.int32), sds((nd, per, 1), jnp.int32)],
        compiler_params=pltpu.CompilerParams(vmem_limit_bytes=VMEM_LIMIT),
    )(meta_all)
    send_tok, send_cot = pl.pallas_call(
        functools.partial(gather_kernel, nd, gpp, rows),
        in_specs=[vmem_spec()] * 3,
        out_specs=[vmem_spec()] * 2,
        out_shape=[sds((gpp, per, width), BF16)] * 2,
        compiler_params=pltpu.CompilerParams(vmem_limit_bytes=VMEM_LIMIT),
    )(loc_all, tokens, cotangent)
    wqkv_shard = jnp.concatenate([w_query, w_key, w_value], axis=1).astype(BF16)
    n_disp = nd + max(nd, gpp * nz) + max(gpp, nd // 4)
    x_in, cot_in, wqkv = comm_call(
        functools.partial(dispatch_kernel, nd, nz, gpp),
        [sds((nd, per, width), BF16), sds((nd // 4, per, width), BF16), sds((nd, slab, 3 * cols), BF16)],
        [dma((n_disp,)), dma((n_disp,)), dma((3,))],
        1,
        (send_tok, send_cot, wqkv_shard),
    )
    x_in = x_in.reshape(rows, width)
    wqkv = wqkv.reshape(width, 3 * cols)
    seg_col = seg_in.reshape(rows, 1)
    seg_row = seg_in.reshape(1, rows)

    qkv = jnp.dot(x_in, wqkv, preferred_element_type=F32)
    scale = jnp.where(jnp.arange(3 * cols) < cols, 0.125, 1.0)
    qkv = ((qkv + jnp.concatenate([bq, jnp.zeros_like(bq), bv])) * scale).astype(BF16)
    mixed, lse = attend(qkv, seg_col, seg_row, heads, 256)

    quad = [dma((3,)), dma((3,))]
    (mixed_in,) = comm_call(
        functools.partial(quad_kernel, nd),
        [sds((4, part, cols), BF16)],
        quad,
        2,
        (mixed.reshape(4, part, cols),),
    )
    residual = lax.dynamic_slice_in_dim(x_in, t * part, part, 0).astype(F32)
    grad_out = cot_in.reshape(part, width).astype(F32)

    attn = jnp.einsum("tri,tdi->rd", mixed_in, out_t, preferred_element_type=F32)
    first_in = residual + attn + b_out
    first_norm = layer_norm(first_in, gain_one, shift_one)
    first_low = first_norm.astype(BF16)
    pre_act = jnp.einsum("rd,zdf->zrf", first_low, up_w, preferred_element_type=F32) + bu[:, None, :]
    hidden_low = exact_gelu(pre_act).astype(BF16)
    mlp = jnp.einsum("zrf,zdf->rd", hidden_low, down_t, preferred_element_type=F32)
    second_in = first_norm + mlp + b_down
    result = layer_norm(second_in, gain_two, shift_two)
    grad_second, gain2_grad, shift2_grad = norm_back(second_in, gain_two, shift_two, grad_out)
    branch_low = grad_second.astype(BF16)
    dbias_grad = jnp.sum(branch_low, axis=0, dtype=F32)
    down_grad = jnp.einsum("rd,zrf->zdf", branch_low, hidden_low, preferred_element_type=F32)
    grad_hidden = jnp.einsum("rd,zdf->zrf", branch_low, down_t, preferred_element_type=F32)
    grad_pre = jax.vjp(exact_gelu, pre_act)[1](grad_hidden)[0].astype(BF16)
    ubias_grad = jnp.sum(grad_pre, axis=1, dtype=F32)
    up_grad = jnp.einsum("rd,zrf->zdf", first_low, grad_pre, preferred_element_type=F32)
    back = jnp.einsum("zrf,zdf->rd", grad_pre, up_w, preferred_element_type=F32)
    grad_first = grad_second + back
    grad_attn_in, gain1_grad, shift1_grad = norm_back(first_in, gain_one, shift_one, grad_first)
    attn_low = grad_attn_in.astype(BF16)
    obias_grad = jnp.sum(attn_low, axis=0, dtype=F32)
    out_grad = jnp.einsum("rd,tri->tdi", attn_low, mixed_in, preferred_element_type=F32)
    grad_mixed = jnp.einsum("rd,tdi->tri", attn_low, out_t, preferred_element_type=F32).astype(BF16)

    w_grads = jnp.concatenate([up_grad, down_grad, out_grad], axis=2).astype(BF16)
    w_grads = lax.psum_scatter(
        w_grads.reshape(nz * width, 2 * ff + cols), ("tensor", "dp"), scatter_dimension=0, tiled=True
    ).astype(F32)

    (grad_in_mixed,) = comm_call(
        functools.partial(quad_kernel, nd), [sds((4, part, cols), BF16)], quad, 3, (grad_mixed,)
    )
    grad_in_mixed = grad_in_mixed.reshape(rows, cols)
    dq, dkv = attend_back(qkv, grad_in_mixed, lse, seg_col, seg_row, heads, 256)
    dqkv = jnp.concatenate([dq, dkv], axis=1)
    bias_sums = jnp.sum(dqkv, axis=0, dtype=F32)
    back_part = jnp.einsum("rc,dc->rd", dqkv, wqkv, preferred_element_type=F32).astype(BF16)
    dw = jnp.einsum("rd,rc->dc", x_in, dqkv, preferred_element_type=F32).astype(BF16)
    mine = (jnp.arange(nz) == t)[:, None]
    vec = jnp.concatenate(
        [
            jnp.where(mine, bias_sums[:cols], 0.0).reshape(-1),
            jnp.where(mine, bias_sums[2 * cols :], 0.0).reshape(-1),
            obias_grad,
            gain1_grad,
            shift1_grad,
            dbias_grad,
            gain2_grad,
            shift2_grad,
            ubias_grad.reshape(-1),
        ]
    ).reshape(-1, 128)
    n_back = 3 + nd + max(nd, nz * gpp)
    part_in, vec_in, dw_in = comm_call(
        functools.partial(back_kernel, nd, nz, gpp),
        [sds((4, part, width), BF16), sds((nd,) + vec.shape, F32), sds((nz * gpp, slab, 3 * cols), BF16)],
        [dma((n_back,)), dma((n_back,)), dma((1,))],
        4,
        (back_part.reshape(4, part, width), vec, dw.reshape(nd, slab, 3 * cols)),
    )
    grad_in = grad_attn_in + jnp.sum(part_in, axis=0, dtype=F32)
    dw_sum = jnp.sum(dw_in, axis=0, dtype=F32)
    vec_plane = jnp.sum(vec_in, axis=0)
    quarter = nd // 4
    block = (quarter, per, width)
    got, got_grad, vec_z = comm_call(
        functools.partial(combine_kernel, nd, nz, gpp, 2),
        [sds((nz, gpp, per, width), BF16)] * 2 + [sds((nz,) + vec.shape, F32)],
        [
            dma((2, quarter)),
            dma((2, gpp)),
            dma((2, nz)),
            dma((2, nz)),
            dma((2, nz)),
            dma((2, nz)),
            dma((nz,)),
            dma((nz,)),
            dma((2,)),
        ],
        5,
        (result.astype(BF16).reshape(block), grad_in.astype(BF16).reshape(block), vec_plane),
    )
    layer_out, grad_tokens = restore(
        loc_all.reshape(1, rows), (got.reshape(rows, width), got_grad.reshape(rows, width)), 256
    )
    vec_all = jnp.sum(vec_z, axis=0).reshape(-1)
    q_all, v_all = vec_all[:width].reshape(nz, cols), vec_all[width : 2 * width].reshape(nz, cols)
    rest = vec_all[2 * width : 8 * width].reshape(6, width)
    u_all = vec_all[8 * width :].reshape(nz, ff)

    def mine_of(array):
        return lax.dynamic_index_in_dim(array, z, 0, keepdims=False)

    return (
        layer_out,
        grad_tokens,
        dw_sum[:, :cols],
        dw_sum[:, cols : 2 * cols],
        dw_sum[:, 2 * cols :],
        mine_of(q_all),
        mine_of(v_all),
        w_grads[:, 2 * ff :].T,
        rest[0],
        rest[1],
        rest[2],
        w_grads[:, :ff],
        mine_of(u_all),
        w_grads[:, ff : 2 * ff].T,
        rest[3],
        rest[4],
        rest[5],
    )


def solution(mesh):
    in_specs = (
        P("dp", None),
        P("dp", None),
        P("dp"),
        P("dp", None),
        P("dp", "tensor"),
        P("dp", "tensor"),
        P("dp", "tensor"),
        P("tensor"),
        P("tensor"),
        P("tensor", "dp"),
        P(),
        P(),
        P(),
        P("dp", "tensor"),
        P("tensor"),
        P("tensor", "dp"),
        P(),
        P(),
        P(),
    )
    out_specs = (
        P("dp", None),
        P("dp", None),
        P("dp", "tensor"),
        P("dp", "tensor"),
        P("dp", "tensor"),
        P("tensor"),
        P("tensor"),
        P("tensor", "dp"),
        P(),
        P(),
        P(),
        P("dp", "tensor"),
        P("tensor"),
        P("tensor", "dp"),
        P(),
        P(),
        P(),
    )
    return jax.shard_map(shards, mesh=mesh, in_specs=in_specs, out_specs=out_specs, check_vma=False)
```

time: 1110 us -> 495 us (0.45)
  waiting for transfers between devices: 625 us -> 0.06 us
  Pallas kernels: 0 us -> 371 us
  blocking collectives: 131 us -> 0 us
  local copies, waits for them, and re-layouts: 95.6 us -> 16.8 us
  matrix products: 120 us -> 55.7 us
  other arithmetic: 88.9 us -> 31.2 us
  starting transfers between devices: 14.3 us -> 0.08 us
    psum x4 -> x0, waiting for transfers between devices: 607 us -> none  [tensor_total(): return lax.psum(partial_sum, 'tensor')]
    pallas_call x0 -> x11, Pallas kernels: none -> 371 us  [the longest x6 292 us: comm_call(): pl.pallas_call(kernel, out_shape=out_shape, in_specs=[vmem_spec()] * len(...]
    dot_general x38 -> x12, matrix products: 118 us -> 55.7 us  [the longest x1 15.4 us: shards(): jnp.einsum('rd,zdf->zrf', first_low, up_w, preferred_element_type=F32)]
    gather x9 -> x0, local copies, waits for them, and re-layouts: 59.9 us -> none  [the longest x1 8.86 us: shards(): grad_tokens = grad_rows.reshape(row_count, feat_width)[restore]]
    all_gather x4 -> x0, blocking collectives: 57.3 us -> none  [the longest x1 28.2 us: shards(): lax.all_gather(w_out.astype(bf16), 'dp', axis=1, tiled=True)]
    all_to_all x2 -> x0, blocking collectives: 42.9 us -> none  [the longest x1 33.2 us: shards(): lax.all_to_all(cotangent[asked_rows].reshape(group_count, per_source, fea...]
    psum x1 -> x0, blocking collectives: 31.1 us -> none  [shards(): lax.psum((qbias_grad, vbias_grad, obias_grad, gain1_grad, shift1_grad, ub...]
    reduce_scatter x5 -> x1, waiting for transfers between devices: 18.4 us -> 0.01 us  [shards(): lax.psum_scatter(w_grads.reshape(nz * width, 2 * ff + cols), ('tensor', '...]
  transfers between devices with their start and end apart: 15 -> 2, of which waited for: 5 -> 0; matrix products, arithmetic and copies ran while one was open for 9% -> 8% of each run, Pallas kernels for 0% -> 76%
where the time goes in v1:
time: 495 us; the launch traced here: 489 us
  Pallas kernels  371 us (75%)
  matrix products  55.7 us (11%)
  other arithmetic  31.2 us (6%)
  local copies, waits for them, and re-layouts  16.8 us (3%)
  between operations  14.9 us (3%)
    pallas_call x6, Pallas kernels, comm_call(): pl.pallas_call(kernel, out_shape=out_shape, in_specs=[vmem_spec()] * len(...  292 us
    pallas_call x1, Pallas kernels, attend_back(): pl.pallas_call(functools.partial(attend_back_kernel, heads, steps), grid=...  35.4 us
    pallas_call x1, Pallas kernels, attend(): pl.pallas_call(functools.partial(attend_kernel, heads), grid=(rows // blo...  20.3 us
    dot_general x1, matrix products, shards(): jnp.einsum('rd,zdf->zrf', first_low, up_w, preferred_element_type=F32)  15.4 us
    pallas_call x1, Pallas kernels, restore(): pl.pallas_call(functools.partial(restore_kernel, count), grid=(rows // bl...  11.6 us
  transfers between devices with their start and end apart: 2, of which 0 were waited for; matrix products, arithmetic and copies ran while one was open for 8% of the time, Pallas kernels for 76%

profile of v1, /device:TPU:0, one launch (start us, length us, event | category | flops | bytes accessed | tf_op | source)
XLA Modules:
  0.0 489.3 jit_solution(9286834424025996423)
XLA Ops:
  15.0 10.8 %shard_map.314 = (s32[8,32,128]{2,1,0:T(8,128)}, f32[4,16,128]{2,1,0:T(8,128)}) custom-call(s32[32,128]{1,0:T(8,128)} %pad_add_fusion.meta_ref, f32[16,128]{1,0:T(8,128)} %pad.13.bias_ref), custom_call_target="tpu_custom_call" | custom-call | tf_op jit(solution)/shard_map/pallas_call | solution.py:57
  26.6 5.5 %shard_map.315 = (s32[8,192,1]{2,1,0:T(8,128)}, s32[8,192,1]{2,1,0:T(8,128)}) custom-call(s32[8,32,128]{2,1,0:T(8,128)} %get-tuple-element.38.meta_ref), custom_call_target="tpu_custom_call" | custom-call | tf_op jit(solution)/shard_map/pallas_call | solution.py:694
  34.3 5.5 %shard_map.316 = (bf16[2,192,768]{2,1,0:T(8,128)(2,1)}, bf16[2,192,768]{2,1,0:T(8,128)(2,1)}) custom-call(s32[8,192,1]{2,1,0:T(8,128)} %get-tuple-element.39.loc_ref, bf16[1536,768]{1,0:T(8,128)(2,1)} %tok_ref.1, bf16[1536,768]{1,0:T(8,128)(2,1)} %cot_ref.1), custom_call_target="tpu_custom_call" | custom-call | tf_op jit(solution)/shard_map/pallas_call | solution.py:701
  40.5 54.0 %shard_map.317 = (bf16[8,192,768]{2,1,0:T(8,128)(2,1)}, bf16[2,192,768]{2,1,0:T(8,128)(2,1)}, bf16[8,96,576]{2,1,0:T(8,128)(2,1)}) custom-call(bf16[2,192,768]{2,1,0:T(8,128)(2,1)} %get-tuple-element.40.tok_ref, bf16[2,192,768]{2,1,0:T(8,128)(2,1)} %get-tuple-element.41.cot_ref, bf16[96,576]{1,0:T(8,128)(2,1)} %pad_maximum_fusion.5.wqkv_ref), custom_call_target="tpu_custom_call" | custom-call | tf_op jit(solution)/shard_map/pallas_call | solution.py:57
  94.7 5.2 %multiply_convert_fusion.q_ref.kv_ref = bf16[1536,576]{1,0:T(8,128)(2,1)} fusion(bf16[1536,768]{1,0:T(8,128)(2,1)} %bitcast.229, bf16[768,576]{1,0:T(8,128)(2,1)} %bitcast.232, f32[576]{0:T(1024)S(1)} %get-tuple-element.152, f32[576]{0:T(1024)S(1)} %get-tuple-element.151), kind=kOutput, calls=%fused_computation.43 | convolution fusion | flops 1361608704 | bytes 5018112 | tf_op jit(solution)/shard_map/dot_general | solution.py:722
  99.9 20.3 %shard_map.318 = (bf16[1536,192]{1,0:T(8,128)(2,1)}, f32[1536,128]{1,0:T(8,128)}) custom-call(bf16[1536,576]{1,0:T(8,128)(2,1)} %multiply_convert_fusion.q_ref.kv_ref, bf16[1536,576]{1,0:T(8,128)(2,1)} %multiply_convert_fusion.q_ref.kv_ref, s32[1536,1]{1,0:T(8,128)} %bitcast.196, s32[1,1536]{1,0:T(1,128)} %reshape.232.segr_ref), custom_call_target="tpu_custom_call" | custom-call | tf_op jit(solution)/shard_map/pallas_call | solution.py:510
  120.2 34.8 %shard_map.319 = bf16[4,384,192]{2,1,0:T(8,128)(2,1)} custom-call(bf16[4,384,192]{2,1,0:T(8,128)(2,1)} %bitcast.209), custom_call_target="tpu_custom_call" | custom-call | tf_op jit(solution)/shard_map/pallas_call | solution.py:57
  155.1 2.9 fusion.82
  158.3 15.4 %fusion.9 = (bf16[4,384,768]{2,1,0:T(8,128)(2,1)S(1)}, f32[4,384,768]{2,1,0:T(8,128)S(1)}, f32[4,768,384]{1,2,0:T(8,128)}) fusion(f32[4,768]{1,0:T(4,128)S(1)} %slice.123, bf16[4,768,1728]{2,1,0:T(8,128)(2,1)} %bitcast.222, f32[384,768]{1,0:T(8,128)S(1)} %get-tuple-element.144, f32[768]{0:T(1024)S(1)} %copy-done.18, f32[768]{0:T(1024)S(1)} %copy-done.13, ...), kind=kOutput, calls=%fused_computation.18 | convolution fusion | flops 1891270656 | bytes 17716224 | tf_op jit(solution)/shard_map/rd,zdf->zrf/dot_general | solution.py:742
  173.7 2.2 fusion.83
  178.4 5.2 %convert_reduce_fusion.1 = (f32[4,768]{1,0:T(4,128)S(1)}, bf16[4,384,768]{2,1,0:T(8,128)(2,1)S(1)}) fusion(f32[4,384,768]{2,1,0:T(8,128)S(1)} %get-tuple-element.124, bf16[4,768,1728]{2,1,0:T(8,128)(2,1)S(1)} %bitcast.227, bf16[384,768]{1,0:T(8,128)(2,1)S(1)} %get-tuple-element.116, f32[4,768,384]{1,2,0:T(8,128)} %get-tuple-element.145, ...), kind=kOutput, calls=%fused_computation.20 | convolution fusion | flops 1831990272 | bytes 17129472 | tf_op jit(solution)/shard_map/rd,zdf->zrf/dot_general | solution.py:751
  183.6 2.4 multiply_reduce_fusion
  186.0 4.6 convolution_convert_fusion.2
  190.6 4.3 convolution_convert_fusion.1
  199.9 9.8 %pad_maximum_fusion = bf16[3072,1728]{1,0:T(8,128)(2,1)} fusion(bf16[3072,192]{1,0:T(8,128)(2,1)S(1)} %bitcast.198, bf16[3072,768]{1,0:T(8,128)(2,1)} %bitcast.200, bf16[3072,768]{1,0:T(8,128)(2,1)} %bitcast.199), kind=kLoop, calls=%fused_computation | loop fusion | flops 31850496 | bytes 21233664 | tf_op jit(solution)/shard_map/concatenate | solution.py:763
  212.0 2.4 fusion.57
  215.6 12.9 %shard_map.320 = bf16[4,384,192]{2,1,0:T(8,128)(2,1)} custom-call(bf16[4,384,192]{2,1,0:T(8,128)(2,1)} %bitcast.203), custom_call_target="tpu_custom_call" | custom-call | tf_op jit(solution)/shard_map/pallas_call | solution.py:57
  228.6 35.4 %shard_map.321 = (bf16[1536,192]{1,0:T(8,128)(2,1)}, bf16[1536,384]{1,0:T(8,128)(2,1)}) custom-call(bf16[1536,576]{1,0:T(8,128)(2,1)} %multiply_convert_fusion.q_ref.kv_ref, bf16[1536,576]{1,0:T(8,128)(2,1)} %multiply_convert_fusion.q_ref.kv_ref, bf16[1536,192]{1,0:T(8,128)(2,1)} %bitcast.202, f32[1536,128]{1,0:T(8,128)} %get-tuple-element.48.lse_ref, ...), custom_call_target="tpu_custom_call" | custom-call | tf_op jit(solution)/shard_map/pallas_call | solution.py:581
  263.9 2.4 convert_reduce_fusion.2
  266.6 4.4 convolution_convert_fusion.4
  272.6 4.9 %convolution_convert_fusion = bf16[1536,768]{1,0:T(8,128)(2,1)} fusion(bf16[768,576]{1,0:T(8,128)(2,1)} %bitcast.233, bf16[1536,384]{1,0:T(8,128)(2,1)S(1)} %copy-done.2, bf16[1536,192]{1,0:T(8,128)(2,1)} %get-tuple-element.49), kind=kOutput, calls=%fused_computation.44 | convolution fusion | flops 1363673088 | bytes 5013504 | tf_op jit(solution)/shard_map/rc,dc->rd/dot_general | solution.py:775
  277.5 75.8 %shard_map.322 = (bf16[4,384,768]{2,1,0:T(8,128)(2,1)}, f32[8,72,128]{2,1,0:T(8,128)}, bf16[8,96,576]{2,1,0:T(8,128)(2,1)}) custom-call(bf16[4,384,768]{2,1,0:T(8,128)(2,1)} %bitcast.208, f32[72,128]{1,0:T(8,128)} %bitcast.213, bf16[8,96,576]{2,1,0:T(8,128)(2,1)} %bitcast.201), custom_call_target="tpu_custom_call" | custom-call | tf_op jit(solution)/shard_map/pallas_call | solution.py:57
  358.2 104.0 %shard_map.323 = (bf16[4,2,192,768]{3,2,1,0:T(8,128)(2,1)}, bf16[4,2,192,768]{3,2,1,0:T(8,128)(2,1)}, f32[4,72,128]{2,1,0:T(8,128)}) custom-call(bf16[2,192,768]{2,1,0:T(8,128)(2,1)} %bitcast.206, bf16[2,192,768]{2,1,0:T(8,128)(2,1)} %bitcast.207, f32[72,128]{1,0:T(8,128)} %reduce_sum.204.refs_2_), custom_call_target="tpu_custom_call" | custom-call | tf_op jit(solution)/shard_map/pallas_call | solution.py:57
  463.9 11.6 %shard_map.324 = (bf16[1536,768]{1,0:T(8,128)(2,1)}, bf16[1536,768]{1,0:T(8,128)(2,1)}) custom-call(s32[1,1536]{1,0:T(1,128)} %reshape.227.loc_ref, bf16[1536,768]{1,0:T(8,128)(2,1)} %bitcast.204, bf16[1536,768]{1,0:T(8,128)(2,1)} %bitcast.205), custom_call_target="tpu_custom_call" | custom-call | tf_op jit(solution)/shard_map/pallas_call | solution.py:620
  (128 shorter events, 37.8 us)
Async XLA Ops:
  7.2 6.4 %copy-start.7 = (f32[96,192]{1,0:T(8,128)S(1)}, f32[96,192]{1,0:T(8,128)}, u32[]{:S(2)}) copy-start(f32[96,192]{1,0:T(8,128)} %param.25) | copy-start | bytes 221188
  7.2 6.4 %copy-start.12 = (f32[768]{0:T(1024)S(1)}, f32[768]{0:T(1024)}, u32[]{:S(2)}) copy-start(f32[768]{0:T(1024)} %param.33) | copy-start | bytes 9220
  7.2 6.4 %copy-start.15 = (f32[192]{0:T(256)S(1)}, f32[192]{0:T(256)}, u32[]{:S(2)}) copy-start(f32[192]{0:T(256)} %param.27) | copy-start | bytes 2308
  7.2 6.4 %copy-start.14 = (f32[192]{0:T(256)S(1)}, f32[192]{0:T(256)}, u32[]{:S(2)}) copy-start(f32[192]{0:T(256)} %param.26) | copy-start | bytes 2308
  7.2 7.1 %copy-start.10 = (s32[1536]{0:T(1024)S(1)}, s32[1536]{0:T(1024)}, u32[]{:S(2)}) copy-start(s32[1536]{0:T(1024)} %param.21) | copy-start | bytes 18436
  7.2 147.8 %all-gather.2.cloned.1.call-start = ((), (), s32[]{:S(2)}) async-start(), calls=%async_computation.1 | async-start | bytes 11354112 | tf_op jit(solution)/shard_map/all_gather | solution.py:667
  11.0 467.1 %reduce-scatter.2.cloned.1.call-start = ((), (), s32[]{:S(2)}) async-start(), calls=%async_computation.2 | async-start | bytes 11354112 | tf_op jit(solution)/shard_map/reduce_scatter | solution.py:764
  99.9 55.1 %copy-start.16 = (f32[768]{0:T(1024)S(1)}, f32[768]{0:T(1024)}, u32[]{:S(2)}) copy-start(f32[768]{0:T(1024)} %param.29) | copy-start | bytes 9220
  155.0 3.2 copy-start.13
  155.1 3.2 copy-start.18
  155.1 18.6 %slice-start = ((s8[11010048]{0:T(1024)(128)(4,1)}), s8[4194304]{0:T(1024)(128)(4,1)S(1)}, s32[]{:S(2)}) async-start(s8[11010048]{0:T(1024)(128)(4,1)} %bitcast.224), calls=%async_computation.3 | async-start | bytes 8388608
  158.2 15.4 %slice-start.1 = ((s8[11010048]{0:T(1024)(128)(4,1)}), s8[4194304]{0:T(1024)(128)(4,1)S(1)}, s32[]{:S(2)}) async-start(s8[11010048]{0:T(1024)(128)(4,1)} %bitcast.224), calls=%async_computation.4 | async-start | bytes 8388608
  158.2 15.4 %slice-start.2 = ((s8[11010048]{0:T(1024)(128)(4,1)}), s8[2621440]{0:T(1024)(128)(4,1)S(1)}, s32[]{:S(2)}) async-start(s8[11010048]{0:T(1024)(128)(4,1)} %bitcast.224), calls=%async_computation.5 | async-start | bytes 5242880
  158.3 15.4 %copy-start.17 = (f32[768]{0:T(1024)S(1)}, f32[768]{0:T(1024)}, u32[]{:S(2)}) copy-start(f32[768]{0:T(1024)} %param.35) | copy-start | bytes 9220
  173.7 2.5 copy-start
  173.7 2.5 copy-start.9
  175.9 0.9 copy-start.11
  194.9 1.5 copy-start.4
  195.6 0.8 copy-start.5
  209.7 1.1 copy-start.1
  209.7 2.3 copy-start.6
  266.6 6.0 %copy-start.2 = (bf16[1536,384]{1,0:T(8,128)(2,1)S(1)}, bf16[1536,384]{1,0:T(8,128)(2,1)}, u32[]{:S(2)}) copy-start(bf16[1536,384]{1,0:T(8,128)(2,1)} %get-tuple-element.50) | copy-start | bytes 3538948
  272.6 4.9 %copy-start.8 = (f32[9216]{0:T(1024)}, f32[9216]{0:T(1024)S(1)}, u32[]{:S(2)}) copy-start(f32[9216]{0:T(1024)S(1)} %constant_dynamic-update-slice_fusion) | copy-start | bytes 110596
  463.9 13.4 %copy-start.3 = (bf16[8,96,576]{2,1,0:T(8,128)(2,1)S(1)}, bf16[8,96,576]{2,1,0:T(8,128)(2,1)}, u32[]{:S(2)}) copy-start(bf16[8,96,576]{2,1,0:T(8,128)(2,1)} %get-tuple-element.57) | copy-start | bytes 2654212
Sparse Core Ops, SparseCore 0:
  11.1 129.1 all-gather.1
  209.9 205.9 reduce-scatter.1

commit v2 on v1

--- a/solution.py
+++ b/solution.py
@@ -13,26 +13,21 @@
 MESH = pl.DeviceIdType.MESH
 F32 = jnp.float32
 BF16 = jnp.bfloat16
+DP = ("pair", "core")
 VMEM_LIMIT = 56 * 1024 * 1024
+
+
+def place():
+    return lax.axis_index("pair") * 2 + lax.axis_index("core"), lax.axis_index("tensor")
+
+
+def at(dp, tensor=None):
+    device = {"pair": dp // 2, "core": lax.rem(dp, 2)}
+    return device if tensor is None else {**device, "tensor": tensor}
 
 
 def vmem_spec():
     return pl.BlockSpec(memory_space=pltpu.VMEM)
-
-
-def layer_norm(rows_in, gain, shift):
-    center = rows_in - jnp.mean(rows_in, axis=-1, keepdims=True)
-    spread = jnp.mean(center * center, axis=-1, keepdims=True)
-    return center * lax.rsqrt(spread + EPSILON) * gain + shift
-
-
-def norm_back(rows_in, gain, shift, upstream):
-    result, pullback = jax.vjp(layer_norm, rows_in, gain, shift)
-    return pullback(upstream)
-
-
-def exact_gelu(values):
-    return jax.nn.gelu(values, approximate=False)
 
 
 def remote(src, dst, send_sem, recv_sem, device):
@@ -53,12 +48,15 @@
     pl.semaphore_wait(barrier, len(devices))
 
 
-def comm_call(kernel, out_shape, scratch, cid, args):
+def comm_call(kernel, out_shape, scratch, cid, args, in_place=0):
+    def specs(count):
+        return [vmem_spec()] * (count - in_place) + [pl.BlockSpec(memory_space=pl.ANY)] * in_place
+
     return pl.pallas_call(
         kernel,
         out_shape=out_shape,
-        in_specs=[vmem_spec()] * len(args),
-        out_specs=[vmem_spec()] * len(out_shape),
+        in_specs=specs(len(args)),
+        out_specs=specs(len(out_shape)),
         scratch_shapes=scratch,
         compiler_params=pltpu.CompilerParams(
             collective_id=cid, has_side_effects=True, vmem_limit_bytes=VMEM_LIMIT
@@ -67,8 +65,8 @@
 
 
 def meta_kernel(nd, nz, meta_ref, bias_ref, meta_out, bias_out, ssem, rsem):
-    d, z = lax.axis_index("dp"), lax.axis_index("tensor")
-    plane = [{"dp": lax.rem(d + k, nd)} for k in range(1, nd)]
+    d, z = place()
+    plane = [at(lax.rem(d + k, nd)) for k in range(1, nd)]
     column = [{"tensor": lax.rem(z + k, nz)} for k in range(1, nz)]
     greet(plane + column)
     copies = []
@@ -87,7 +85,7 @@
 
 def index_kernel(nd, gpp, rows, meta_ref, loc_ref, seg_ref):
     per = rows // nd
-    d, z = lax.axis_index("dp"), lax.axis_index("tensor")
+    d, z = place()
     group = z * gpp + d // 4
     lane_i = lax.broadcasted_iota(jnp.int32, (128, 128), 0)
     lane_j = lax.broadcasted_iota(jnp.int32, (128, 128), 1)
@@ -121,7 +119,7 @@
 
 def gather_kernel(nd, gpp, rows, loc_ref, tok_ref, cot_ref, tok_out, cot_out):
     per = rows // nd
-    z = lax.axis_index("tensor")
+    _, z = place()
     column = lax.broadcasted_iota(jnp.int32, (per, rows), 1)
     for k in range(gpp):
         loc = loc_ref[z * gpp + k]
@@ -133,20 +131,20 @@
 def dispatch_kernel(
     nd, nz, gpp, tok_ref, cot_ref, wqkv_ref, x_out, cot_out, w_out, ssem, rsem, lsem
 ):
-    d, z = lax.axis_index("dp"), lax.axis_index("tensor")
+    d, z = place()
     t = lax.rem(d, 4)
     quarter = nd // 4
     everyone = []
     for kz in range(nz):
         for kd in range(nd):
             if kz or kd:
-                everyone.append({"dp": lax.rem(d + kd, nd), "tensor": lax.rem(z + kz, nz)})
+                everyone.append(at(lax.rem(d + kd, nd), lax.rem(z + kz, nz)))
     greet(everyone)
     waits = []
     locals_ = []
     for k in range(1, nd):
         dest = lax.rem(d + k, nd)
-        copy = remote(tok_ref.at[dest // 4], x_out.at[d], ssem.at[k], rsem.at[k], {"dp": dest})
+        copy = remote(tok_ref.at[dest // 4], x_out.at[d], ssem.at[k], rsem.at[k], at(dest))
         copy.start()
         waits.append(copy)
     own = pltpu.make_async_copy(tok_ref.at[d // 4], x_out.at[d], lsem.at[0])
@@ -162,7 +160,7 @@
                 w_out.at[d],
                 ssem.at[base + m * nz + kz],
                 rsem.at[base + d],
-                {"dp": dest, "tensor": dz},
+                at(dest, dz),
             )
             if kz == 0:
 
@@ -183,7 +181,7 @@
             cot_out.at[lax.rem(d, quarter)],
             ssem.at[base_c + k],
             rsem.at[base_c + lax.rem(d, quarter)],
-            {"dp": dest},
+            at(dest),
         )
 
         @pl.when(dest != d)
@@ -208,7 +206,7 @@
                 w_out.at[d],
                 ssem.at[base + m * nz + kz],
                 rsem.at[base + d],
-                {"dp": dest, "tensor": lax.rem(z + kz, nz)},
+                at(dest, lax.rem(z + kz, nz)),
             )
             if kz == 0:
 
@@ -223,7 +221,7 @@
                 send.wait_send()
     for s in range(nd):
         came = remote(
-            wqkv_ref, w_out.at[s], ssem.at[base], rsem.at[base + s], {"dp": s, "tensor": t}
+            wqkv_ref, w_out.at[s], ssem.at[base], rsem.at[base + s], at(s, t)
         )
 
         @pl.when(jnp.logical_or(t != z, d != s))
@@ -237,7 +235,7 @@
             cot_out.at[lax.rem(d, quarter)],
             ssem.at[base_c + k],
             rsem.at[base_c + lax.rem(d, quarter)],
-            {"dp": dest},
+            at(dest),
         )
 
         @pl.when(dest != d)
@@ -253,7 +251,7 @@
     for j in range(quarter):
         source = t * quarter + j
         came = remote(
-            cot_ref.at[0], cot_out.at[j], ssem.at[base_c], rsem.at[base_c + j], {"dp": source}
+            cot_ref.at[0], cot_out.at[j], ssem.at[base_c], rsem.at[base_c + j], at(source)
         )
 
         @pl.when(source != d)
@@ -261,17 +259,19 @@
             came.wait_recv()
 
 
-def quad_kernel(nd, in_ref, out_ref, ssem, rsem):
-    d = lax.axis_index("dp")
+def quad_kernel(in_ref, big_ref, out_ref, big_out, ssem, rsem):
+    d, _ = place()
     t = lax.rem(d, 4)
     first = d - t
     peers = [lax.rem(t + k, 4) for k in range(1, 4)]
-    greet([{"dp": first + peer} for peer in peers])
+    greet([at(first + peer) for peer in peers])
+    core = lax.rem(t, 2)
     copies = []
     for i, peer in enumerate(peers):
         copies.append(
-            remote(in_ref.at[peer], out_ref.at[t], ssem.at[i], rsem.at[i], {"dp": first + peer})
-        )
+            remote(in_ref.at[peer], out_ref.at[t], ssem.at[i], rsem.at[i], at(first + peer))
+        )
+    copies.append(remote(big_ref, big_out, ssem.at[3], rsem.at[3], at(d + 1 - 2 * core)))
     for copy in copies:
         copy.start()
     out_ref[t] = in_ref[t]
@@ -279,98 +279,44 @@
         copy.wait()
 
 
-def back_kernel(
-    nd, nz, gpp, part_ref, vec_ref, dw_ref, part_out, vec_out, dw_out, ssem, rsem, lsem
-):
-    d, z = lax.axis_index("dp"), lax.axis_index("tensor")
+def back_kernel(nd, gpp, part_ref, vec_ref, dw_ref, part_out, vec_out, dw_out, ssem, rsem):
+    d, _ = place()
     t = lax.rem(d, 4)
-    first = d - t
+    group = d // 4
+    greet([at(lax.rem(d + k, nd)) for k in range(1, nd)])
+    other = d - t + lax.rem(t + 2, 4)
+    copies = [remote(part_ref.at[1 - t // 2], part_out, ssem.at[0], rsem.at[0], at(other))]
+    for k in range(1, gpp):
+        peer = lax.rem(group + k, gpp)
+        copies.append(
+            remote(dw_ref.at[peer], dw_out.at[group], ssem.at[k], rsem.at[k], at(4 * peer + t))
+        )
+    for k in range(1, nd):
+        i = gpp + k
+        copies.append(
+            remote(vec_ref, vec_out.at[d], ssem.at[i], rsem.at[i], at(lax.rem(d + k, nd)))
+        )
+    for copy in copies:
+        copy.start()
+    dw_out[group] = dw_ref[group]
+    vec_out[d] = vec_ref[...]
+    for copy in copies:
+        copy.wait()
+
+
+def combine_kernel(nd, nz, gpp, count, *refs):
+    row_refs, (vec_ref, dw_ref) = refs[:count], refs[count : count + 2]
+    outs, (vec_out, dw_out) = refs[count + 2 : 2 * count + 2], refs[2 * count + 2 : 2 * count + 4]
+    ssem, rsem, usend, urecv, dsend, drecv, vsend, vrecv, wsend, wrecv, lsem = refs[2 * count + 4 :]
+    d, z = place()
+    t = lax.rem(d, 4)
+    quarter = nd // 4
     everyone = []
     for kz in range(nz):
         for kd in range(nd):
             if kz or kd:
-                everyone.append({"dp": lax.rem(d + kd, nd), "tensor": lax.rem(z + kz, nz)})
+                everyone.append(at(lax.rem(d + kd, nd), lax.rem(z + kz, nz)))
     greet(everyone)
-    copies = []
-    for k in range(1, 4):
-        peer = lax.rem(t + k, 4)
-        copies.append(
-            remote(part_ref.at[peer], part_out.at[t], ssem.at[k], rsem.at[k], {"dp": first + peer})
-        )
-    for k in range(1, nd):
-        copies.append(
-            remote(vec_ref, vec_out.at[d], ssem.at[3 + k], rsem.at[3 + k], {"dp": lax.rem(d + k, nd)})
-        )
-    for copy in copies:
-        copy.start()
-    base = 3 + nd
-    slot = z * gpp + d // 4
-
-    def send_dw(k):
-        dest = lax.rem(d + k, nd)
-        return remote(
-            dw_ref.at[dest],
-            dw_out.at[slot],
-            ssem.at[base + k],
-            rsem.at[base + slot],
-            {"dp": dest, "tensor": t},
-        )
-
-    own = pltpu.make_async_copy(dw_ref.at[d], dw_out.at[slot], lsem.at[0])
-    for k in range(nd):
-        if k == 0:
-
-            @pl.when(t != z)
-            def _():
-                send_dw(0).start()
-
-            @pl.when(t == z)
-            def _():
-                own.start()
-        else:
-            send_dw(k).start()
-    part_out[t] = part_ref[t]
-    vec_out[d] = vec_ref[...]
-    for copy in copies:
-        copy.wait()
-    for k in range(nd):
-        if k == 0:
-
-            @pl.when(t != z)
-            def _():
-                send_dw(0).wait_send()
-
-            @pl.when(t == z)
-            def _():
-                own.wait()
-        else:
-            send_dw(k).wait_send()
-    for sz in range(nz):
-        for k in range(gpp):
-            source = 4 * k + z
-            came = remote(
-                dw_ref.at[0],
-                dw_out.at[sz * gpp + k],
-                ssem.at[base],
-                rsem.at[base + sz * gpp + k],
-                {"dp": source, "tensor": sz},
-            )
-
-            @pl.when(jnp.logical_or(source != d, z != sz))
-            def _():
-                came.wait_recv()
-
-
-def combine_kernel(nd, nz, gpp, count, *refs):
-    row_refs, (vec_ref,) = refs[:count], refs[count : count + 1]
-    outs, (vec_out,) = refs[count + 1 : 2 * count + 1], refs[2 * count + 1 : 2 * count + 2]
-    ssem, rsem, usend, urecv, dsend, drecv, vsend, vrecv, lsem = refs[2 * count + 2 :]
-    d, z = lax.axis_index("dp"), lax.axis_index("tensor")
-    t = lax.rem(d, 4)
-    quarter = nd // 4
-    plane = [{"dp": lax.rem(d + k, nd)} for k in range(1, nd)]
-    column = [{"tensor": lax.rem(z + k, nz)} for k in range(1, nz)]
-    greet(plane + column)
     vecs = []
     for k in range(1, nz):
         copy = remote(vec_ref, vec_out.at[z], vsend.at[k], vrecv.at[k], {"tensor": lax.rem(z + k, nz)})
@@ -385,7 +331,7 @@
                 outs[i].at[z, d // 4],
                 ssem.at[i, b],
                 rsem.at[i, d // 4],
-                {"dp": dest},
+                at(dest),
             )
             own = pltpu.make_async_copy(row_refs[i].at[b], outs[i].at[z, d // 4], lsem.at[i])
 
@@ -396,6 +342,24 @@
             @pl.when(dest == d)
             def _():
                 own.start()
+
+    own_dw = pltpu.make_async_copy(dw_ref.at[t], dw_out.at[z], lsem.at[count])
+
+    def send_dw(j):
+        return remote(
+            dw_ref.at[j], dw_out.at[z], wsend.at[j], wrecv.at[z], at(d - t + j, t)
+        )
+
+    for j in range(4):
+        mine = (j == t) & (t == z)
+
+        @pl.when(jnp.logical_not(mine))
+        def _():
+            send_dw(j).start()
+
+        @pl.when(mine)
+        def _():
+            own_dw.start()
 
     def hop(i, k, up):
         block = z - k if up else z + k
@@ -424,7 +388,7 @@
         for k in range(gpp):
             source = 4 * k + d // quarter
             arrive = remote(
-                row_refs[i].at[0], outs[i].at[z, k], ssem.at[i, 0], rsem.at[i, k], {"dp": source}
+                row_refs[i].at[0], outs[i].at[z, k], ssem.at[i, 0], rsem.at[i, k], at(source)
             )
 
             @pl.when(source != d)
@@ -471,12 +435,33 @@
                 outs[i].at[z, d // 4],
                 ssem.at[i, b],
                 rsem.at[i, d // 4],
-                {"dp": dest},
+                at(dest),
             )
 
             @pl.when(dest != d)
             def _():
                 copy.wait_send()
+
+    for j in range(4):
+        mine = (j == t) & (t == z)
+
+        @pl.when(jnp.logical_not(mine))
+        def _():
+            send_dw(j).wait_send()
+
+        @pl.when(mine)
+        def _():
+            own_dw.wait()
+
+    for sz in range(nz):
+        source = d - t + z
+        came_dw = remote(
+            dw_ref.at[0], dw_out.at[sz], wsend.at[0], wrecv.at[sz], at(source, sz)
+        )
+
+        @pl.when(jnp.logical_or(source != d, z != sz))
+        def _():
+            came_dw.wait_recv()
 
     for copy in vecs:
         copy.wait()
@@ -605,6 +590,161 @@
     )(qkv, qkv, grad, lse, seg_col, seg_row)
 
 
+def norm_parts(rows_in):
+    center = rows_in - jnp.mean(rows_in, axis=-1, keepdims=True)
+    spread = jnp.mean(center * center, axis=-1, keepdims=True)
+    scale = lax.rsqrt(spread + EPSILON)
+    return center * scale, scale
+
+
+def norm_grad(normed, scale, gain, upstream):
+    e = upstream * gain
+    mean_e = jnp.mean(e, axis=-1, keepdims=True)
+    mean_en = jnp.mean(e * normed, axis=-1, keepdims=True)
+    return scale * (e - mean_e - normed * mean_en)
+
+
+def dot_nt(left, right):
+    return lax.dot_general(left, right, (((1,), (1,)), ((), ())), preferred_element_type=F32)
+
+
+def dot_nn(left, right):
+    return jnp.dot(left, right, preferred_element_type=F32)
+
+
+def rowwise_kernel(
+    nz,
+    half,
+    x_ref,
+    mix_ref,
+    cot_ref,
+    own_ref,
+    oth_ref,
+    bu_ref,
+    par_ref,
+    res_ref,
+    gin_ref,
+    gmix_ref,
+    down_ref,
+    doth_ref,
+    ub_ref,
+    vec_ref,
+    slope_s,
+    hid_s,
+    acc_s,
+    first_s,
+    first_t,
+    branch_t,
+    norm_s,
+):
+    core = lax.axis_index("core")
+    halves = ((own_ref, down_ref), (oth_ref, doth_ref))
+    out0, out1 = 2 * half, 2 * half + mix_ref.shape[2] // 2
+    mid = mix_ref.shape[2] // 2
+    b_out, gain1, shift1 = par_ref[0:1, :], par_ref[1:2, :], par_ref[2:3, :]
+    b_down, gain2, shift2 = par_ref[3:4, :], par_ref[4:5, :], par_ref[5:6, :]
+
+    def mix_halves(q):
+        low, high = mix_ref[q, :, 0:mid], mix_ref[q, :, mid : 2 * mid]
+        return jnp.where(core == 0, low, high), jnp.where(core == 0, high, low)
+
+    total = x_ref[...].astype(F32) + b_out
+    for q in range(nz):
+        for part, (weights, _) in zip(mix_halves(q), halves):
+            total = total + dot_nt(part, weights[q, :, out0:out1])
+    normed1, scale1 = norm_parts(total)
+    norm_s[...] = normed1
+    first_norm = normed1 * gain1 + shift1
+    first_low = first_norm.astype(BF16)
+    first_s[...] = first_low
+    first_t[...] = first_norm.T.astype(BF16)
+    acc_s[...] = first_norm + b_down
+
+    def forward(q, carry):
+        for h, (weights, _) in enumerate(halves):
+            pre = dot_nn(first_s[...], weights[q, :, 0:half]) + bu_ref[q, h : h + 1, :]
+            phi_cum = 0.5 + 0.5 * lax.erf(pre * (0.5**0.5))
+            density = jnp.exp(-0.5 * pre * pre) * 0.3989422804014327
+            hidden = (pre * phi_cum).astype(BF16)
+            slope_s[q, h] = phi_cum + pre * density
+            hid_s[q, h] = hidden
+            acc_s[...] += dot_nt(hidden, weights[q, :, half : 2 * half])
+        return carry
+
+    lax.fori_loop(0, nz, forward, 0)
+    normed2, scale2 = norm_parts(acc_s[...])
+    res_ref[...] = (normed2 * gain2 + shift2).astype(BF16)
+    upstream = cot_ref[...].astype(F32)
+    vec_ref[4:5, :] = jnp.sum(upstream * normed2, axis=0, keepdims=True)
+    vec_ref[5:6, :] = jnp.sum(upstream, axis=0, keepdims=True)
+    grad_second = norm_grad(normed2, scale2, gain2, upstream)
+    branch_low = grad_second.astype(BF16)
+    vec_ref[3:4, :] = jnp.sum(branch_low.astype(F32), axis=0, keepdims=True)
+    branch_t[...] = grad_second.T.astype(BF16)
+    res_b = branch_low
+    acc_s[...] = grad_second
+
+    def backward(q, carry):
+        for h, (weights, grads) in enumerate(halves):
+            grad_hidden = dot_nn(res_b, weights[q, :, half : 2 * half])
+            grad_pre = (grad_hidden * slope_s[q, h]).astype(BF16)
+            ub_ref[q, h : h + 1, :] = jnp.sum(grad_pre.astype(F32), axis=0, keepdims=True)
+            acc_s[...] += dot_nt(grad_pre, weights[q, :, 0:half])
+            grads[q, :, 0:half] = dot_nn(first_t[...], grad_pre).astype(BF16)
+            grads[q, :, half : 2 * half] = dot_nn(branch_t[...], hid_s[q, h]).astype(BF16)
+        return carry
+
+    lax.fori_loop(0, nz, backward, 0)
+    grad_first = acc_s[...]
+    vec_ref[1:2, :] = jnp.sum(grad_first * norm_s[...], axis=0, keepdims=True)
+    vec_ref[2:3, :] = jnp.sum(grad_first, axis=0, keepdims=True)
+    grad_in = norm_grad(norm_s[...], scale1, gain1, grad_first)
+    gin_ref[...] = grad_in
+    attn_low = grad_in.astype(BF16)
+    vec_ref[0:1, :] = jnp.sum(attn_low.astype(F32), axis=0, keepdims=True)
+    vec_ref[6:8, :] = jnp.zeros((2, vec_ref.shape[1]), F32)
+    attn_t = grad_in.T.astype(BF16)
+    for q in range(nz):
+        back = []
+        for part, (weights, grads) in zip(mix_halves(q), halves):
+            grads[q, :, out0:out1] = dot_nn(attn_t, part).astype(BF16)
+            back.append(dot_nn(attn_low, weights[q, :, out0:out1]).astype(BF16))
+        low = jnp.where(core == 0, back[0], back[1])
+        high = jnp.where(core == 0, back[1], back[0])
+        gmix_ref[q] = jnp.concatenate([low, high], axis=1)
+
+
+def rowwise(x, mixed, cot, own, oth, bu, params):
+    rows, width = x.shape
+    nz, cols = mixed.shape[0], mixed.shape[2]
+    half = bu.shape[2]
+    sds = jax.ShapeDtypeStruct
+    return pl.pallas_call(
+        functools.partial(rowwise_kernel, nz, half),
+        in_specs=[vmem_spec()] * 7,
+        out_specs=[vmem_spec()] * 7,
+        out_shape=[
+            sds((rows, width), BF16),
+            sds((rows, width), F32),
+            sds((nz, rows, cols), BF16),
+            sds(own.shape, BF16),
+            sds(own.shape, BF16),
+            sds((nz, 2, half), F32),
+            sds((8, width), F32),
+        ],
+        scratch_shapes=[
+            pltpu.VMEM((nz, 2, rows, half), F32),
+            pltpu.VMEM((nz, 2, rows, half), BF16),
+            pltpu.VMEM((rows, width), F32),
+            pltpu.VMEM((rows, width), BF16),
+            pltpu.VMEM((width, rows), BF16),
+            pltpu.VMEM((width, rows), BF16),
+            pltpu.VMEM((rows, width), F32),
+        ],
+        compiler_params=pltpu.CompilerParams(vmem_limit_bytes=VMEM_LIMIT),
+    )(x, mixed, cot, own, oth, bu, params)
+
+
 def restore_kernel(count, loc_ref, *refs):
     ins, outs = refs[:count], refs[count:]
     block = outs[0].shape[0]
@@ -649,7 +789,7 @@
     gain_two,
     shift_two,
 ):
-    nd, nz = lax.axis_size("dp"), lax.axis_size("tensor")
+    nd, nz = lax.axis_size("pair") * 2, lax.axis_size("tensor")
     rows, width = tokens.shape
     gpp = nd // 4
     per = rows // nd
@@ -658,15 +798,39 @@
     cols = w_query.shape[1]
     heads = cols // HEAD_DIM
     ff = w_up.shape[1]
-    d, z = lax.axis_index("dp"), lax.axis_index("tensor")
+    d, z = place()
     t = d % 4
     sds = jax.ShapeDtypeStruct
     dma = pltpu.SemaphoreType.DMA
 
-    shard = jnp.concatenate([w_up, w_down.T, w_out.T], axis=1).astype(BF16)
-    whole = lax.all_gather(shard, ("tensor", "dp"), axis=0, tiled=True)
-    whole = whole.reshape(nz, width, 2 * ff + cols)
-    up_w, down_t, out_t = whole[:, :, :ff], whole[:, :, ff : 2 * ff], whole[:, :, 2 * ff :]
+    core = lax.axis_index("core")
+    swap = [(0, 1), (1, 0)]
+
+    def pick(array, index, axis=0):
+        return lax.dynamic_index_in_dim(array, index, axis, keepdims=False)
+
+    half, mid = ff // 2, cols // 2
+    down_t, out_t = w_down.T, w_out.T
+    pieces = jnp.stack(
+        [
+            jnp.concatenate(
+                [
+                    w_up[:, h * half : (h + 1) * half],
+                    down_t[:, h * half : (h + 1) * half],
+                    out_t[:, h * mid : (h + 1) * mid],
+                ],
+                axis=1,
+            )
+            for h in range(2)
+        ]
+    ).astype(BF16)
+    got_piece = lax.ppermute(pick(pieces, 1 - core), "core", swap)
+    kept = pick(pieces, core)
+    shard = jnp.concatenate(
+        [jnp.where(core == 0, kept, got_piece), jnp.where(core == 0, got_piece, kept)]
+    )
+    own_w = lax.all_gather(shard, ("tensor", "pair"), axis=0, tiled=True)
+    own_w = own_w.reshape(nz, width, 2 * half + mid)
 
     pad = 16 - rows // 128
     meta = jnp.concatenate(
@@ -689,7 +853,8 @@
     bias_all = bias_all[:, :bias_rows].reshape(nz, bias_rows * 128)
     own_bias = lax.dynamic_index_in_dim(bias_all, t, 0, keepdims=False)
     bq, bv = own_bias[:cols], own_bias[cols : 2 * cols]
-    bu = bias_all[:, 2 * cols :]
+    bu = bias_all[:, 2 * cols :].reshape(nz, 2, half)
+    bu = jnp.where(core == 0, bu, bu[:, ::-1])
 
     loc_all, seg_in = pl.pallas_call(
         functools.partial(index_kernel, nd, gpp, rows),
@@ -724,86 +889,82 @@
     qkv = ((qkv + jnp.concatenate([bq, jnp.zeros_like(bq), bv])) * scale).astype(BF16)
     mixed, lse = attend(qkv, seg_col, seg_row, heads, 256)
 
-    quad = [dma((3,)), dma((3,))]
-    (mixed_in,) = comm_call(
-        functools.partial(quad_kernel, nd),
-        [sds((4, part, cols), BF16)],
+    quad = [dma((4,)), dma((4,))]
+    mixed_in, oth_w = comm_call(
+        quad_kernel,
+        [sds((4, part, cols), BF16), sds(own_w.shape, BF16)],
         quad,
         2,
-        (mixed.reshape(4, part, cols),),
-    )
-    residual = lax.dynamic_slice_in_dim(x_in, t * part, part, 0).astype(F32)
-    grad_out = cot_in.reshape(part, width).astype(F32)
-
-    attn = jnp.einsum("tri,tdi->rd", mixed_in, out_t, preferred_element_type=F32)
-    first_in = residual + attn + b_out
-    first_norm = layer_norm(first_in, gain_one, shift_one)
-    first_low = first_norm.astype(BF16)
-    pre_act = jnp.einsum("rd,zdf->zrf", first_low, up_w, preferred_element_type=F32) + bu[:, None, :]
-    hidden_low = exact_gelu(pre_act).astype(BF16)
-    mlp = jnp.einsum("zrf,zdf->rd", hidden_low, down_t, preferred_element_type=F32)
-    second_in = first_norm + mlp + b_down
-    result = layer_norm(second_in, gain_two, shift_two)
-    grad_second, gain2_grad, shift2_grad = norm_back(second_in, gain_two, shift_two, grad_out)
-    branch_low = grad_second.astype(BF16)
-    dbias_grad = jnp.sum(branch_low, axis=0, dtype=F32)
-    down_grad = jnp.einsum("rd,zrf->zdf", branch_low, hidden_low, preferred_element_type=F32)
-    grad_hidden = jnp.einsum("rd,zdf->zrf", branch_low, down_t, preferred_element_type=F32)
-    grad_pre = jax.vjp(exact_gelu, pre_act)[1](grad_hidden)[0].astype(BF16)
-    ubias_grad = jnp.sum(grad_pre, axis=1, dtype=F32)
-    up_grad = jnp.einsum("rd,zrf->zdf", first_low, grad_pre, preferred_element_type=F32)
-    back = jnp.einsum("zrf,zdf->rd", grad_pre, up_w, preferred_element_type=F32)
-    grad_first = grad_second + back
-    grad_attn_in, gain1_grad, shift1_grad = norm_back(first_in, gain_one, shift_one, grad_first)
-    attn_low = grad_attn_in.astype(BF16)
-    obias_grad = jnp.sum(attn_low, axis=0, dtype=F32)
-    out_grad = jnp.einsum("rd,tri->tdi", attn_low, mixed_in, preferred_element_type=F32)
-    grad_mixed = jnp.einsum("rd,tdi->tri", attn_low, out_t, preferred_element_type=F32).astype(BF16)
-
-    w_grads = jnp.concatenate([up_grad, down_grad, out_grad], axis=2).astype(BF16)
+        (mixed.reshape(4, part, cols), own_w),
+        in_place=1,
+    )
+    residual = lax.dynamic_slice_in_dim(x_in, t * part, part, 0)
+    zero = jnp.zeros_like(b_out)
+    params = jnp.stack([b_out, gain_one, shift_one, b_down, gain_two, shift_two, zero, zero])
+    result, grad_attn_in, grad_mixed, dw_own, dw_oth, ubias_grad, sums = rowwise(
+        residual, mixed_in, cot_in.reshape(part, width), own_w, oth_w, bu, params
+    )
+    ubias_grad = jnp.where(core == 0, ubias_grad, ubias_grad[:, ::-1])
+    grad_in_mixed, dw_got = comm_call(
+        quad_kernel,
+        [sds((4, part, cols), BF16), sds(dw_oth.shape, BF16)],
+        quad,
+        3,
+        (grad_mixed, dw_oth),
+        in_place=1,
+    )
     w_grads = lax.psum_scatter(
-        w_grads.reshape(nz * width, 2 * ff + cols), ("tensor", "dp"), scatter_dimension=0, tiled=True
-    ).astype(F32)
-
-    (grad_in_mixed,) = comm_call(
-        functools.partial(quad_kernel, nd), [sds((4, part, cols), BF16)], quad, 3, (grad_mixed,)
-    )
+        (dw_own + dw_got).reshape(nz * width, 2 * half + mid),
+        ("tensor", "pair"),
+        scatter_dimension=0,
+        tiled=True,
+    ).reshape(2, slab, 2 * half + mid)
+    g_kept = pick(w_grads, core).astype(F32)
+    g_got = lax.ppermute(pick(w_grads, 1 - core), "core", swap).astype(F32)
+    g_low, g_high = jnp.where(core == 0, g_kept, g_got), jnp.where(core == 0, g_got, g_kept)
+    up_grad = jnp.concatenate([g_low[:, :half], g_high[:, :half]], axis=1)
+    down_grad = jnp.concatenate([g_low[:, half : 2 * half], g_high[:, half : 2 * half]], axis=1).T
+    out_grad = jnp.concatenate([g_low[:, 2 * half :], g_high[:, 2 * half :]], axis=1).T
+
     grad_in_mixed = grad_in_mixed.reshape(rows, cols)
     dq, dkv = attend_back(qkv, grad_in_mixed, lse, seg_col, seg_row, heads, 256)
     dqkv = jnp.concatenate([dq, dkv], axis=1)
     bias_sums = jnp.sum(dqkv, axis=0, dtype=F32)
     back_part = jnp.einsum("rc,dc->rd", dqkv, wqkv, preferred_element_type=F32).astype(BF16)
     dw = jnp.einsum("rd,rc->dc", x_in, dqkv, preferred_element_type=F32).astype(BF16)
+    back_part = back_part.reshape(2, 2, part, width)
+    part_got = lax.ppermute(pick(back_part, 1 - core, 1), "core", swap)
+    part_sum = pick(back_part, core, 1).astype(F32) + part_got.astype(F32)
     mine = (jnp.arange(nz) == t)[:, None]
     vec = jnp.concatenate(
         [
             jnp.where(mine, bias_sums[:cols], 0.0).reshape(-1),
             jnp.where(mine, bias_sums[2 * cols :], 0.0).reshape(-1),
-            obias_grad,
-            gain1_grad,
-            shift1_grad,
-            dbias_grad,
-            gain2_grad,
-            shift2_grad,
+            sums[:6].reshape(-1),
             ubias_grad.reshape(-1),
         ]
     ).reshape(-1, 128)
-    n_back = 3 + nd + max(nd, nz * gpp)
+    n_back = gpp + nd
     part_in, vec_in, dw_in = comm_call(
-        functools.partial(back_kernel, nd, nz, gpp),
-        [sds((4, part, width), BF16), sds((nd,) + vec.shape, F32), sds((nz * gpp, slab, 3 * cols), BF16)],
-        [dma((n_back,)), dma((n_back,)), dma((1,))],
+        functools.partial(back_kernel, nd, gpp),
+        [
+            sds((part, width), BF16),
+            sds((nd,) + vec.shape, F32),
+            sds((gpp, 4, slab, 3 * cols), BF16),
+        ],
+        [dma((n_back,)), dma((n_back,))],
         4,
-        (back_part.reshape(4, part, width), vec, dw.reshape(nd, slab, 3 * cols)),
-    )
-    grad_in = grad_attn_in + jnp.sum(part_in, axis=0, dtype=F32)
-    dw_sum = jnp.sum(dw_in, axis=0, dtype=F32)
+        (part_sum.astype(BF16), vec, dw.reshape(gpp, 4, slab, 3 * cols)),
+    )
+    grad_in = grad_attn_in + pick(part_sum, t // 2) + part_in.astype(F32)
+    dw_low = jnp.sum(dw_in, axis=0, dtype=F32).astype(BF16)
     vec_plane = jnp.sum(vec_in, axis=0)
     quarter = nd // 4
     block = (quarter, per, width)
-    got, got_grad, vec_z = comm_call(
+    got, got_grad, vec_z, dw_z = comm_call(
         functools.partial(combine_kernel, nd, nz, gpp, 2),
-        [sds((nz, gpp, per, width), BF16)] * 2 + [sds((nz,) + vec.shape, F32)],
+        [sds((nz, gpp, per, width), BF16)] * 2
+        + [sds((nz,) + vec.shape, F32), sds((nz, slab, 3 * cols), BF16)],
         [
             dma((2, quarter)),
             dma((2, gpp)),
@@ -813,11 +974,14 @@
             dma((2, nz)),
             dma((nz,)),
             dma((nz,)),
-            dma((2,)),
+            dma((4,)),
+            dma((nz,)),
+            dma((3,)),
         ],
         5,
-        (result.astype(BF16).reshape(block), grad_in.astype(BF16).reshape(block), vec_plane),
-    )
+        (result.reshape(block), grad_in.astype(BF16).reshape(block), vec_plane, dw_low),
+    )
+    dw_sum = jnp.sum(dw_z, axis=0, dtype=F32)
     layer_out, grad_tokens = restore(
         loc_all.reshape(1, rows), (got.reshape(rows, width), got_grad.reshape(rows, width)), 256
     )
@@ -825,9 +989,6 @@
     q_all, v_all = vec_all[:width].reshape(nz, cols), vec_all[width : 2 * width].reshape(nz, cols)
     rest = vec_all[2 * width : 8 * width].reshape(6, width)
     u_all = vec_all[8 * width :].reshape(nz, ff)
-
-    def mine_of(array):
-        return lax.dynamic_index_in_dim(array, z, 0, keepdims=False)
 
     return (
         layer_out,
@@ -835,15 +996,15 @@
         dw_sum[:, :cols],
         dw_sum[:, cols : 2 * cols],
         dw_sum[:, 2 * cols :],
-        mine_of(q_all),
-        mine_of(v_all),
-        w_grads[:, 2 * ff :].T,
+        pick(q_all, z),
+        pick(v_all, z),
+        out_grad,
         rest[0],
         rest[1],
         rest[2],
-        w_grads[:, :ff],
-        mine_of(u_all),
-        w_grads[:, ff : 2 * ff].T,
+        up_grad,
+        pick(u_all, z),
+        down_grad,
         rest[3],
         rest[4],
         rest[5],
@@ -851,42 +1012,44 @@
 
 
 def solution(mesh):
+    split = (mesh.shape["dp"] // 2, 2, mesh.shape["tensor"])
+    mesh = jax.sharding.Mesh(mesh.devices.reshape(split), ("pair", "core", "tensor"))
     in_specs = (
-        P("dp", None),
-        P("dp", None),
-        P("dp"),
-        P("dp", None),
-        P("dp", "tensor"),
-        P("dp", "tensor"),
-        P("dp", "tensor"),
+        P(DP, None),
+        P(DP, None),
+        P(DP),
+        P(DP, None),
+        P(DP, "tensor"),
+        P(DP, "tensor"),
+        P(DP, "tensor"),
         P("tensor"),
         P("tensor"),
-        P("tensor", "dp"),
-        P(),
-        P(),
-        P(),
-        P("dp", "tensor"),
+        P("tensor", DP),
+        P(),
+        P(),
+        P(),
+        P(DP, "tensor"),
         P("tensor"),
-        P("tensor", "dp"),
+        P("tensor", DP),
         P(),
         P(),
         P(),
     )
     out_specs = (
-        P("dp", None),
-        P("dp", None),
-        P("dp", "tensor"),
-        P("dp", "tensor"),
-        P("dp", "tensor"),
+        P(DP, None),
+        P(DP, None),
+        P(DP, "tensor"),
+        P(DP, "tensor"),
+        P(DP, "tensor"),
         P("tensor"),
         P("tensor"),
-        P("tensor", "dp"),
-        P(),
-        P(),
-        P(),
-        P("dp", "tensor"),
+        P("tensor", DP),
+        P(),
+        P(),
+        P(),
+        P(DP, "tensor"),
         P("tensor"),
-        P("tensor", "dp"),
+        P("tensor", DP),
         P(),
         P(),
         P(),

time: 495 us -> 470 us (0.949)
  matrix products: 55.7 us -> 13.6 us
  waiting for transfers between devices: 0.06 us -> 19.4 us
  Pallas kernels: 371 us -> 362 us
  local copies, waits for them, and re-layouts: 16.8 us -> 22.1 us
    dot_general x9 -> x0, matrix products: 41.2 us -> none  [the longest x1 15.4 us: shards(): jnp.einsum('rd,zdf->zrf', first_low, up_w, preferred_element_type=F32)]
    all_gather x1, waiting for transfers between devices: 0.02 us -> 18.3 us  [shards(): own_w = lax.all_gather(shard, ('tensor', 'pair'), axis=0, tiled=True)]
    concatenate x2, other arithmetic: 10.6 us -> 1.49 us  [the longest x1 0.76 us: shards(): jnp.concatenate([jnp.where(core == 0, kept, got_piece), jnp.where(core ==...]
    pallas_call x6 -> x7, Pallas kernels: 292 us -> 284 us  [the longest x6 250 us: comm_call(): pl.pallas_call(kernel, out_shape=out_shape, in_specs=specs(len(args)), ou...]
    add x0 -> x1, other arithmetic: none -> 6.27 us  [shards(): dw_own + dw_got]
  transfers between devices with their start and end apart: 2 -> 5, of which waited for: 0 -> 2; matrix products, arithmetic and copies ran while one was open for 8% -> 11% of each run, Pallas kernels for 76% -> 64%
where the time goes in v2:
time: 470 us; the launch traced here: 464 us
  Pallas kernels  362 us (77%)
  other arithmetic  30.1 us (6%)
  local copies, waits for them, and re-layouts  22.1 us (5%)
  waiting for transfers between devices  19.4 us (4%)
  between operations  15.1 us (3%)
  matrix products  13.6 us (3%)
    pallas_call x6, Pallas kernels, comm_call(): pl.pallas_call(kernel, out_shape=out_shape, in_specs=specs(len(args)), ou...  250 us
    pallas_call x1, Pallas kernels, attend_back(): pl.pallas_call(functools.partial(attend_back_kernel, heads, steps), grid=...  35.5 us
    pallas_call x1, Pallas kernels, rowwise(): pl.pallas_call(functools.partial(rowwise_kernel, nz, half), in_specs=[vme...  34.3 us
    pallas_call x1, Pallas kernels, attend(): pl.pallas_call(functools.partial(attend_kernel, heads), grid=(rows // blo...  20.3 us
    all_gather x1, waiting for transfers between devices, shards(): own_w = lax.all_gather(shard, ('tensor', 'pair'), axis=0, tiled=True)  18.3 us
    pallas_call x1, Pallas kernels, restore(): pl.pallas_call(functools.partial(restore_kernel, count), grid=(rows // bl...  11.6 us
  transfers between devices with their start and end apart: 5, of which 2 were waited for; matrix products, arithmetic and copies ran while one was open for 11% of the time, Pallas kernels for 64%

profile of v2, /device:TPU:0, one launch (start us, length us, event | category | flops | bytes accessed | tf_op | source)
XLA Modules:
  0.0 464.0 jit_solution(15173973173457739345)
XLA Ops:
  14.9 10.7 %shard_map.314 = (s32[8,32,128]{2,1,0:T(8,128)}, f32[4,16,128]{2,1,0:T(8,128)}) custom-call(s32[32,128]{1,0:T(8,128)} %pad_add_fusion.meta_ref, f32[16,128]{1,0:T(8,128)} %pad.13.bias_ref), custom_call_target="tpu_custom_call" | custom-call | tf_op jit(solution)/shard_map/pallas_call | solution.py:55
  26.5 5.5 %shard_map.315 = (s32[8,192,1]{2,1,0:T(8,128)}, s32[8,192,1]{2,1,0:T(8,128)}) custom-call(s32[8,32,128]{2,1,0:T(8,128)} %get-tuple-element.50.meta_ref), custom_call_target="tpu_custom_call" | custom-call | tf_op jit(solution)/shard_map/pallas_call | solution.py:859
  34.2 5.5 %shard_map.316 = (bf16[2,192,768]{2,1,0:T(8,128)(2,1)}, bf16[2,192,768]{2,1,0:T(8,128)(2,1)}) custom-call(s32[8,192,1]{2,1,0:T(8,128)} %get-tuple-element.51.loc_ref, bf16[1536,768]{1,0:T(8,128)(2,1)} %tok_ref.1, bf16[1536,768]{1,0:T(8,128)(2,1)} %cot_ref.1), custom_call_target="tpu_custom_call" | custom-call | tf_op jit(solution)/shard_map/pallas_call | solution.py:866
  40.5 51.4 %shard_map.317 = (bf16[8,192,768]{2,1,0:T(8,128)(2,1)}, bf16[2,192,768]{2,1,0:T(8,128)(2,1)}, bf16[8,96,576]{2,1,0:T(8,128)(2,1)}) custom-call(bf16[2,192,768]{2,1,0:T(8,128)(2,1)} %get-tuple-element.52.tok_ref, bf16[2,192,768]{2,1,0:T(8,128)(2,1)} %get-tuple-element.53.cot_ref, bf16[96,576]{1,0:T(8,128)(2,1)} %pad_maximum_fusion.5.wqkv_ref), custom_call_target="tpu_custom_call" | custom-call | tf_op jit(solution)/shard_map/pallas_call | solution.py:55
  92.0 5.2 %multiply_convert_fusion.q_ref.kv_ref = bf16[1536,576]{1,0:T(8,128)(2,1)} fusion(bf16[1536,768]{1,0:T(8,128)(2,1)} %bitcast.111, bf16[768,576]{1,0:T(8,128)(2,1)} %bitcast.130, f32[576]{0:T(1024)S(1)} %get-tuple-element.151, f32[576]{0:T(1024)S(1)} %get-tuple-element.150), kind=kOutput, calls=%fused_computation.1 | convolution fusion | flops 1361608704 | bytes 5018112 | tf_op jit(solution)/shard_map/dot_general | solution.py:887
  97.2 20.3 %shard_map.318 = (bf16[1536,192]{1,0:T(8,128)(2,1)}, f32[1536,128]{1,0:T(8,128)}) custom-call(bf16[1536,576]{1,0:T(8,128)(2,1)} %multiply_convert_fusion.q_ref.kv_ref, bf16[1536,576]{1,0:T(8,128)(2,1)} %multiply_convert_fusion.q_ref.kv_ref, s32[1536,1]{1,0:T(8,128)} %bitcast.96, s32[1,1536]{1,0:T(1,128)} %reshape.174.segr_ref), custom_call_target="tpu_custom_call" | custom-call | tf_op jit(solution)/shard_map/pallas_call | solution.py:495
  118.1 1.9 constant_dynamic-slice_fusion.4.x_ref
  120.6 18.3 %all-gather.2.cloned.1.call-done = bf16[3072,864]{1,0:T(8,128)(2,1)} async-done(((bf16[192,864]{1,0:T(8,128)(2,1)}), bf16[3072,864]{1,0:T(8,128)(2,1)}) %all-gather.2.cloned.1.call-update) | async-done | bytes 5308432 | tf_op jit(solution)/shard_map/all_gather | solution.py:832
  138.9 18.1 %shard_map.319 = (bf16[4,384,192]{2,1,0:T(8,128)(2,1)}, bf16[4,768,864]{2,1,0:T(8,128)(2,1)}) custom-call(bf16[4,384,192]{2,1,0:T(8,128)(2,1)} %bitcast.105, bf16[4,768,864]{2,1,0:T(8,128)(2,1)} %bitcast.94), custom_call_target="tpu_custom_call" | custom-call | tf_op jit(solution)/shard_map/pallas_call | solution.py:55
  157.0 34.3 %shard_map.320 = (bf16[384,768]{1,0:T(8,128)(2,1)}, f32[384,768]{1,0:T(8,128)}, bf16[4,384,192]{2,1,0:T(8,128)(2,1)}, bf16[4,768,864]{2,1,0:T(8,128)(2,1)}, bf16...) custom-call(bf16[384,768]{1,0:T(8,128)(2,1)} %constant_dynamic-slice_fusion.4.x_ref, ...), custom_call_target="tpu_custom_call" | custom-call | tf_op jit(solution)/shard_map/pallas_call | solution.py:722
  191.2 13.1 %shard_map.321 = (bf16[4,384,192]{2,1,0:T(8,128)(2,1)}, bf16[4,768,864]{2,1,0:T(8,128)(2,1)}) custom-call(bf16[4,384,192]{2,1,0:T(8,128)(2,1)} %get-tuple-element.64.in_ref, bf16[4,768,864]{2,1,0:T(8,128)(2,1)} %get-tuple-element.65.big_ref), custom_call_target="tpu_custom_call" | custom-call | tf_op jit(solution)/shard_map/pallas_call | solution.py:55
  204.3 6.3 %add.80 = bf16[4,768,864]{2,1,0:T(8,128)(2,1)} add(bf16[4,768,864]{2,1,0:T(8,128)(2,1)S(1)} %copy-done, bf16[4,768,864]{2,1,0:T(8,128)(2,1)} %get-tuple-element.82) | non-fusion elementwise | flops 2654208 | bytes 15925248 | tf_op jit(solution)/shard_map/add | solution.py:917
  214.0 35.5 %shard_map.322 = (bf16[1536,192]{1,0:T(8,128)(2,1)}, bf16[1536,384]{1,0:T(8,128)(2,1)}) custom-call(bf16[1536,576]{1,0:T(8,128)(2,1)} %multiply_convert_fusion.q_ref.kv_ref, bf16[1536,576]{1,0:T(8,128)(2,1)} %multiply_convert_fusion.q_ref.kv_ref, bf16[1536,192]{1,0:T(8,128)(2,1)} %bitcast.104, f32[1536,128]{1,0:T(8,128)} %get-tuple-element.67.lse_ref, ...), custom_call_target="tpu_custom_call" | custom-call | tf_op jit(solution)/shard_map/pallas_call | solution.py:566
  249.6 3.6 convolution_convert_fusion
  257.9 2.0 convert_reduce_fusion
  262.8 4.9 %convolution_convert_fusion.1 = bf16[768,576]{0,1:T(8,128)(2,1)} fusion(bf16[1536,768]{1,0:T(8,128)(2,1)} %bitcast.113, bf16[1536,384]{1,0:T(8,128)(2,1)S(1)} %copy-done.3, bf16[1536,192]{1,0:T(8,128)(2,1)} %get-tuple-element.68), kind=kOutput, calls=%fused_computation.5 | convolution fusion | flops 1362935808 | bytes 5013504 | tf_op jit(solution)/shard_map/rd,rc->dc/dot_general | solution.py:934
  267.6 2.2 copy.43
  271.2 2.6 fusion.10
  273.8 29.0 %shard_map.323 = (bf16[384,768]{1,0:T(8,128)(2,1)}, f32[8,72,128]{2,1,0:T(8,128)}, bf16[2,4,96,576]{3,2,1,0:T(8,128)(2,1)}) custom-call(bf16[2,384,768]{2,1,0:T(8,128)(2,1)} %get-tuple-element.117.part_ref, f32[72,128]{1,0:T(8,128)} %maximum_bitcast_fusion.4.vec_ref, bf16[2,4,96,576]{3,2,1,0:T(8,128)(2,1)} %bitcast.98), custom_call_target="tpu_custom_call" | custom-call | tf_op jit(solution)/shard_map/pallas_call | solution.py:55
  302.9 1.6 reduce_sum.49.refs_2_
  304.5 2.3 reduce_sum.50.refs_3_
  306.8 2.1 fusion.1
  308.9 127.4 %shard_map.324 = (bf16[4,2,192,768]{3,2,1,0:T(8,128)(2,1)}, bf16[4,2,192,768]{3,2,1,0:T(8,128)(2,1)}, f32[4,72,128]{2,1,0:T(8,128)}, bf16[4,96,576]{2,1,0:T(8,128)(2,1)}) custom-call(bf16[2,192,768]{2,1,0:T(8,128)(2,1)} %bitcast.107, bf16[2,192,768]{2,1,0:T(8,128)(2,1)} %bitcast.103, f32[72,128]{1,0:T(8,128)} %reduce_sum.49.refs_2_, ...), custom_call_target="tpu_custom_call" | custom-call | tf_op jit(solution)/shard_map/pallas_call | solution.py:55
  441.5 11.6 %shard_map.325 = (bf16[1536,768]{1,0:T(8,128)(2,1)}, bf16[1536,768]{1,0:T(8,128)(2,1)}) custom-call(s32[1,1536]{1,0:T(1,128)} %reshape.169.loc_ref, bf16[1536,768]{1,0:T(8,128)(2,1)} %bitcast.99, bf16[1536,768]{1,0:T(8,128)(2,1)} %bitcast.100), custom_call_target="tpu_custom_call" | custom-call | tf_op jit(solution)/shard_map/pallas_call | solution.py:760
  (128 shorter events, 33.5 us)
Async XLA Ops:
  7.2 131.7 %all-gather.2.cloned.1.call-start = ((), (), s32[]{:S(2)}) async-start(), calls=%async_computation.1 | async-start | bytes 5849088 | tf_op jit(solution)/shard_map/all_gather | solution.py:832
  8.2 5.1 %copy-start.14 = (f32[768]{0:T(1024)S(1)}, f32[768]{0:T(1024)}, u32[]{:S(2)}) copy-start(f32[768]{0:T(1024)} %param.29) | copy-start | bytes 9220
  8.2 5.1 %copy-start.15 = (f32[768]{0:T(1024)S(1)}, f32[768]{0:T(1024)}, u32[]{:S(2)}) copy-start(f32[768]{0:T(1024)} %param.30) | copy-start | bytes 9220
  8.3 5.1 %copy-start.16 = (f32[768]{0:T(1024)S(1)}, f32[768]{0:T(1024)}, u32[]{:S(2)}) copy-start(f32[768]{0:T(1024)} %param.31) | copy-start | bytes 9220
  8.3 5.0 %copy-start.17 = (f32[768]{0:T(1024)S(1)}, f32[768]{0:T(1024)}, u32[]{:S(2)}) copy-start(f32[768]{0:T(1024)} %param.35) | copy-start | bytes 9220
  8.4 5.0 %copy-start.18 = (f32[768]{0:T(1024)S(1)}, f32[768]{0:T(1024)}, u32[]{:S(2)}) copy-start(f32[768]{0:T(1024)} %param.36) | copy-start | bytes 9220
  8.4 5.0 %copy-start.19 = (f32[768]{0:T(1024)S(1)}, f32[768]{0:T(1024)}, u32[]{:S(2)}) copy-start(f32[768]{0:T(1024)} %param.37) | copy-start | bytes 9220
  8.4 5.0 %copy-start.12 = (s32[1,1536]{1,0:T(1,128)S(1)}, s32[1,1536]{1,0:T(1,128)}, u32[]{:S(2)}) copy-start(s32[1,1536]{1,0:T(1,128)} %param.22) | copy-start | bytes 18436
  8.4 5.1 %copy-start.6 = (f32[96,192]{1,0:T(8,128)S(1)}, f32[96,192]{1,0:T(8,128)}, u32[]{:S(2)}) copy-start(f32[96,192]{1,0:T(8,128)} %param.23) | copy-start | bytes 221188
  8.4 5.1 %copy-start.7 = (f32[96,192]{1,0:T(8,128)S(1)}, f32[96,192]{1,0:T(8,128)}, u32[]{:S(2)}) copy-start(f32[96,192]{1,0:T(8,128)} %param.24) | copy-start | bytes 221188
  9.4 4.1 copy-start.8
  9.5 4.1 copy-start.13
  9.5 4.1 copy-start.20
  9.5 4.1 copy-start.21
  9.5 4.7 %copy-start.11 = (s32[1536]{0:T(1024)S(1)}, s32[1536]{0:T(1024)}, u32[]{:S(2)}) copy-start(s32[1536]{0:T(1024)} %param.21) | copy-start | bytes 18436
  10.7 1.6 collective-permute-start
  13.2 426.6 %reduce-scatter.2.cloned.1.call-start = ((), (), s32[]{:S(2)}) async-start(), calls=%async_computation.2 | async-start | bytes 5849088 | tf_op jit(solution)/shard_map/reduce_scatter | solution.py:916
  191.2 13.1 %copy-start = (bf16[4,768,864]{2,1,0:T(8,128)(2,1)S(1)}, bf16[4,768,864]{2,1,0:T(8,128)(2,1)}, u32[]{:S(2)}) copy-start(bf16[4,768,864]{2,1,0:T(8,128)(2,1)} %get-tuple-element.81) | copy-start | bytes 15925252
  214.0 35.6 %copy-start.22 = (bf16[8,96,576]{2,1,0:T(8,128)(2,1)S(1)}, bf16[8,96,576]{2,1,0:T(8,128)(2,1)}, u32[]{:S(2)}) copy-start(bf16[8,96,576]{2,1,0:T(8,128)(2,1)} %get-tuple-element.55) | copy-start | bytes 2654212
  253.2 4.7 %copy-start.3 = (bf16[1536,384]{1,0:T(8,128)(2,1)S(1)}, bf16[1536,384]{1,0:T(8,128)(2,1)}, u32[]{:S(2)}) copy-start(bf16[1536,384]{1,0:T(8,128)(2,1)} %get-tuple-element.69) | copy-start | bytes 3538948
  254.7 16.6 %collective-permute-start.1 = (bf16[2,384,768]{2,1,0:T(8,128)(2,1)S(1)}, bf16[2,384,768]{2,1,0:T(8,128)(2,1)S(1)}, u32[]{:S(2)}, u32[]{:S(2)}) collective-permute-start(bf16[2,384,768]{2,1,0:T(8,128)(2,1)S(1)} %dynamic-slice_bitcast_fusion), channel_id=1, source_target_pairs={{0,4},{4,0},{1,5},{5,1},{2,6},{6,2},{3,7},{7,3},{8,12},{12,8},{9,1... | collective-permute-start | bytes 3538952 | tf_op jit(solution)/shard_map/ppermute | solution.py:936
  273.8 33.0 %copy-start.4 = (f32[384,768]{1,0:T(8,128)S(1)}, f32[384,768]{1,0:T(8,128)}, u32[]{:S(2)}) copy-start(f32[384,768]{1,0:T(8,128)} %get-tuple-element.63) | copy-start | bytes 3538948
  440.8 13.5 %collective-permute-start.2 = (bf16[96,864]{1,0:T(8,128)(2,1)S(1)}, bf16[96,864]{1,0:T(8,128)(2,1)S(1)}, u32[]{:S(2)}, u32[]{:S(2)}) collective-permute-start(bf16[96,864]{1,0:T(8,128)(2,1)S(1)} %dynamic-slice_bitcast_fusion.1), channel_id=1, source_target_pairs={{0,4},{4,0},{1,5},{5,1},{2,6},{6,2},{3,7},{7,3},{8,12},{12,8},{9,1... | collective-permute-start | bytes 497672 | tf_op jit(solution)/shard_map/ppermute | solution.py:923
  441.5 12.8 %copy-start.5 = (bf16[192,864]{1,0:T(8,128)(2,1)S(1)}, bf16[192,864]{1,0:T(8,128)(2,1)}, u32[]{:S(2)}) copy-start(bf16[192,864]{1,0:T(8,128)(2,1)} %reduce-scatter.2.cloned.1.call-done) | copy-start | bytes 995332
  (4 other events, 6.8 us)
Sparse Core Ops, SparseCore 0:
  13.3 125.5 all-gather.1
  210.8 168.9 reduce-scatter.1
